TPU v7x, 256 devices: a whole 4x4x8 slice. The times are simulated.
256 devices in a mesh: batch: 8 (over y, x_lo), train: 32 (over z, x_hi, core).
Axes of the slice: x: 4 (x_hi: 2, x_lo: 2; x = x_hi * 2 + x_lo), y: 4, z: 8, core: 2. Of those that a mesh axis runs over, the one named last changes fastest.
Arguments:
- batch_rows: int32 [2, 8192], replicated, may hold values from 0 to 131071, as said below
- train_embed: bfloat16 [131072, 256], P('train'), may hold values from -6 to 6
- lib_embed: bfloat16 [8192, 256], P('batch'), may hold values from -6 to 6
- labels: float32 [131072], P('train'), may hold values from -6 to 6
- prior_draws: float32 [32, 131072], P(None, 'train'), may hold values from -6 to 6
- noise_draws: float32 [32, 131072], P(None, 'train'), may hold values from -6 to 6
- coefficients: float32 [33, 131072], P(None, 'train'), may hold values from -4 to 4
- velocity: float32 [33, 131072], P(None, 'train'), may hold values from -1.6 to 1.6
- library_prior: float32 [32, 8192], P(None, ('batch', 'train')), may hold values from -6 to 6
Outputs:
- new_coefficients: float32 [33, 131072], P(None, 'train')
- new_velocity: float32 [33, 131072], P(None, 'train')
- predictions: float32 [33, 8192], P(None, ('batch', 'train'))
Inputs may be any that keep to these rules, and one draw needn't show every extreme that they name: `batch_rows`: each step's 8192 rows are distinct. A step's positions fall into runs of 32; run number q holds rows of the range starting at (q % 32) * 4096 of length 4096.
All inputs are finite; a program needn't handle non-finite values.
Results may differ from a plain program's by a relative error of at most 0.009.
Values may be sent and summed in bfloat16 or wider, within the bound.
No kernel may reach another device: no remote copies, remote signals or barrier semaphores. Data moves between devices by JAX's collectives and lax.ppermute only.
A program may use at most 64 MiB of HBM per device.

v0:
```python
import jax
import jax.numpy as jnp
from jax import lax
from jax.experimental import pallas as pl
from jax.experimental.pallas import tpu as pltpu
from jax.sharding import PartitionSpec as P


momentum = 0.9
step_rate = 0.1
noise_var = 0.5
noise_scale = 0.7071067811865476
length_sq = 0.088

BETA = (5.0 / (length_sq * 256)) ** 0.5
SCALE = BETA * BETA / 3.0
C1 = 3.0 / BETA
C0 = 3.0 / (BETA * BETA)
RATE = BETA * 1.4426950408889634

CARRY = momentum + momentum * momentum
CUT = step_rate * (1.0 + momentum)

COLS = 33
HALF = 64
KEYS = 4096
QUERIES = 1024
TILE = 512
f32 = jnp.float32
bf16 = jnp.bfloat16

GRANT = 20 << 20


def call(body, ins, outs, scratch=(), flops=0):
    spec = {"H": pl.BlockSpec(memory_space=pltpu.HBM), "V": pl.BlockSpec(memory_space=pltpu.VMEM)}
    spec["P"] = spec["V"]
    spec["A"] = pl.BlockSpec(memory_space=pl.ANY)
    space = {"H": pltpu.HBM, "V": pltpu.VMEM, "P": pltpu.HBM, "A": pl.ANY}
    kernel = pl.pallas_call(
        body,
        out_shape=[space[kind](shape, dtype) for kind, shape, dtype in outs],
        in_specs=[spec[kind] for kind, _ in ins],
        out_specs=[spec[kind] for kind, _, _ in outs],
        scratch_shapes=list(scratch),
        compiler_params=pltpu.CompilerParams(vmem_limit_bytes=GRANT),
        cost_estimate=pl.CostEstimate(flops=flops, transcendentals=0, bytes_accessed=1 << 20),
    )
    result = kernel(*[pltpu.with_memory_space_constraint(array, space[kind]) for kind, array in ins])
    return result[0] if len(outs) == 1 else result


def places():
    return lax.axis_index("batch"), lax.axis_index("train")


def dot_nt(left, right):
    return lax.dot_general(left, right, (((1,), (1,)), ((), ())), preferred_element_type=f32)


def dot_nn(left, right):
    return jnp.dot(left, right, preferred_element_type=f32)


def two_terms(x):
    high = x.astype(bf16)
    return high, (x - high.astype(f32)).astype(bf16)


def norms_down(x):
    return jnp.sum(jnp.square(x.astype(f32)), axis=1, keepdims=True)


def norms_across(x):
    high, low = two_terms(jnp.square(x.astype(f32)))
    ones = jnp.ones((8, x.shape[1]), bf16)
    return (dot_nt(ones, high) + dot_nt(ones, low))[0:1]


def matern(cross, norms_q, norms_k):
    dist = jnp.maximum((norms_q + norms_k) + cross, 1e-12)
    root = dist * lax.rsqrt(dist)
    return ((root * (root + C1) + C0) * jnp.exp2(root * -RATE)).astype(bf16)


def local_rows(rows_ref, train, groups):
    chunks = []
    for step in range(2):
        for group in groups:
            start = group * QUERIES + (train // 4) * 128
            chunks.append(rows_ref[pl.ds(step, 1), pl.ds(pl.multiple_of(start, 128), 128)])
    while len(chunks) % 8:
        chunks.append(chunks[0])
    stack = jnp.concatenate(chunks, axis=0)
    stack = pltpu.roll(stack, lax.rem(128 - (train % 4) * 32, 128), axis=1)
    return stack - train * KEYS


def one_hot(column, start, width):
    lanes = lax.broadcasted_iota(jnp.int32, (column.shape[0], width), 1)
    return (lanes == column - start).astype(bf16)


def side_by_side(x):
    return jnp.concatenate([x[0:16], x[16:32]], axis=1)


def one_below_other(x):
    return jnp.concatenate([x[:, 0:HALF], x[:, HALF:]], axis=0)


def pack(total, out_ref):
    for place in range(32):
        out_ref[place] = side_by_side(total[32 * place : 32 * place + 32]).astype(bf16)


def pack_flipped(total, train, flips, out_ref):
    own = lax.rem(train, 4)
    for index, flip in enumerate(flips):
        other = lax.bitwise_xor(own, flip)
        for z in range(8):
            start = 256 * index + 32 * z
            out_ref[4 * z + other] = (SCALE * side_by_side(total[start : start + 32])).astype(bf16)


def pick_body(rows_hbm, embed_hbm, sent_hbm, rows, embed, picked, sems):
    batch, train = places()
    fetch = pltpu.make_async_copy(rows_hbm, rows, sems.at[0])
    fetch.start()
    chunks = []
    for index in range(4):
        part = pl.ds(1024 * index, 1024)
        chunks.append(pltpu.make_async_copy(embed_hbm.at[part], embed.at[part], sems.at[1 + index]))
        chunks[-1].start()
    fetch.wait()
    local = jnp.transpose(local_rows(rows, train, [batch]))
    column = jnp.concatenate([local[0:32, 0:1], local[0:32, 1:2]], axis=0)
    total = jnp.zeros((64, 256), f32)
    for index in range(4):
        chosen = one_hot(column, 1024 * index, 1024)
        chunks[index].wait()
        total = total + dot_nn(chosen, embed[1024 * index : 1024 * index + 1024, :])
    picked[0] = total[0:32].astype(bf16)
    picked[1] = total[32:64].astype(bf16)
    out = [pltpu.make_async_copy(picked, sent_hbm.at[z], sems.at[5 + z]) for z in range(8)]
    for copy in out:
        copy.start()
    for copy in out:
        copy.wait()


def prep_body(
    rows_ref, embed_hbm, labels_hbm, prior_hbm, noise_hbm, coef_hbm, vel_hbm,
    ahead_hbm, base_hbm, own_ref, norms_ref,
    embed, labels, prior, noise, coef, vel, ahead_half, base_half, sems,
):
    batch, train = places()
    copies = [
        pltpu.make_async_copy(source, target, sems.at[index])
        for index, (source, target) in enumerate(
            [
                (coef_hbm, coef), (vel_hbm, vel), (prior_hbm, prior), (noise_hbm, noise), (labels_hbm, labels),
                (embed_hbm, embed),
            ]
        )
    ]
    for copy in copies:
        copy.start()
    mine = jnp.transpose(local_rows(rows_ref, train, [batch]))
    for copy in copies[:2]:
        copy.wait()
    ahead = coef[...] + momentum * vel[...]
    base = coef[...] + CARRY * vel[...]
    pad = jnp.zeros((HALF - COLS, KEYS), f32)
    ahead_half[...] = jnp.concatenate([ahead, pad], axis=0).astype(bf16)
    base_half[...] = jnp.concatenate([base, pad], axis=0).astype(bf16)
    out = [
        pltpu.make_async_copy(ahead_half, ahead_hbm, sems.at[6]),
        pltpu.make_async_copy(base_half, base_hbm, sems.at[7]),
    ]
    for copy in out:
        copy.start()
    for copy in copies[2:]:
        copy.wait()
    shift = jnp.concatenate([jnp.zeros((1, KEYS), f32), prior[...] + noise_scale * noise[...]], axis=0)
    targets = labels[...] - shift
    for step, state in enumerate((ahead, base)):
        chosen = one_hot(mine[0:32, step : step + 1], 0, KEYS)
        high, low = two_terms(jnp.concatenate([noise_var * state - targets, pad], axis=0))
        own_ref[step] = side_by_side(dot_nt(chosen, high) + dot_nt(chosen, low))
    norms_ref[...] = norms_across(embed[...])
    for copy in out:
        copy.wait()


def dense_scratch(queries):
    return [
        pltpu.VMEM((KEYS, 256), bf16),
        pltpu.VMEM((queries, 256), bf16),
        pltpu.VMEM((HALF, KEYS), bf16),
        pltpu.VMEM((queries, 1), f32),
        pltpu.VMEM((2, queries, TILE), f32),
        pltpu.VMEM((queries, HALF), f32),
        pltpu.SemaphoreType.DMA((13,)),
    ]


def dense(embed_hbm, pieces, weight_hbm, norms_ref, scratch, tiles, start_ref=None, short=False):
    embed, query, weight, query_norms, cross, total_ref, sems = scratch
    first, count = tiles

    def chunk(index):
        part = pl.ds(pl.multiple_of((first + index) * TILE, TILE), TILE)
        return pltpu.make_async_copy(embed_hbm.at[part], embed.at[part], sems.at[index])

    rows = query.shape[0] // len(pieces)
    fetches = [
        pltpu.make_async_copy(piece, query.at[pl.ds(rows * index, rows)], sems.at[9 + index])
        for index, piece in enumerate(pieces)
    ]
    fetch_weight = pltpu.make_async_copy(weight_hbm, weight, sems.at[8])
    for fetch in fetches:
        fetch.start()
    chunk(0).start()
    fetch_weight.start()
    for index in range(1, count):
        chunk(index).start()
    total_ref[...] = jnp.zeros_like(total_ref) if start_ref is None else start_ref[...]
    for index, fetch in enumerate(fetches):
        fetch.wait()
        part = slice(rows * index, rows * index + rows)
        query_norms[part, :] = norms_down(query[part, :])
        query[part, :] = query[part, :] * bf16(-2)

    def keys(index):
        return pl.ds(pl.multiple_of((first + index) * TILE, TILE), TILE)

    def product(index):
        return dot_nt(query[...], embed[keys(index), :])

    chunk(0).wait()
    cross[0] = product(0)
    fetch_weight.wait()

    def one(index, slot, more):
        if more:
            cross[1 - slot] = product(jnp.minimum(index + 1, count - 1) if short else index + 1)
        value = matern(cross[slot], query_norms[...], norms_ref[:, keys(index)])
        total_ref[...] += dot_nt(value, weight[:, keys(index)])

    def pair(index, carry):
        chunk(2 * index + 1).wait()
        if short:

            @pl.when(2 * index + 2 < count)
            def _():
                chunk(2 * index + 2).wait()

            one(2 * index, 0, True)
            one(2 * index + 1, 1, True)
        else:
            chunk(2 * index + 2).wait()
            one(2 * index, 0, True)
            one(2 * index + 1, 1, True)
        return carry

    if short:
        lax.fori_loop(0, count // 2, pair, 0)
        return total_ref
    loops = (count - 1) // 2
    lax.fori_loop(0, loops, pair, 0)
    for index in range(2 * loops, count):
        more = index + 1 < count
        if more:
            chunk(index + 1).wait()
        one(index, index % 2, more)
    return total_ref


def dense_first_body(embed, own, flip, weight, norms_ref, after, out_ref, *scratch):
    del after
    total = dense(embed, [own, flip], weight, norms_ref, scratch, (0, 8))
    for index in range(16):
        out_ref[index] = (SCALE * side_by_side(total[32 * index : 32 * index + 32])).astype(bf16)


def dense_rest_body(embed, flip_2, flip_3, weight, norms_ref, done_ref, out_ref, *scratch):
    train = places()[1]
    total = dense(embed, [flip_2, flip_3], weight, norms_ref, scratch, (0, 8))
    pack_flipped(total, train, (2, 3), out_ref)
    own = lax.rem(train, 4)
    for index in range(2):
        other = lax.bitwise_xor(own, index)
        for z in range(8):
            out_ref[4 * z + other] = done_ref[8 * index + z]


def dense_second_body(embed, flip_0, flip_1, flip_2, flip_3, weight, norms_ref, after, out_ref, *scratch):
    del after
    total = dense(embed, [flip_0, flip_1, flip_2, flip_3], weight, norms_ref, scratch, (0, 8))
    pack_flipped(total, places()[1], range(4), out_ref)


LIBRARY_SPLIT = 4


def library_first_body(embed, query, weight, norms_ref, after, out_ref, *scratch):
    del after
    total = dense(embed, [query], weight, norms_ref, scratch, (0, LIBRARY_SPLIT), short=True)
    out_ref[...] = total[...]


def library_second_body(embed, query, weight, norms_ref, start_ref, after, out_ref, *scratch):
    del after
    total = dense(embed, [query], weight, norms_ref, scratch, (LIBRARY_SPLIT, 8 - LIBRARY_SPLIT), start_ref, True)
    out_ref[...] = total[...]


def near_body(rows_ref, embed_hbm, library_hbm, after, near, picks, local_ref, embed, library, sems):
    del after
    copies = [
        pltpu.make_async_copy(embed_hbm, embed, sems.at[0]),
        pltpu.make_async_copy(library_hbm, library, sems.at[1]),
    ]
    for copy in copies:
        copy.start()
    train = places()[1]
    local = jnp.transpose(local_rows(rows_ref, train, range(8)))
    local_ref[...] = local
    column = jnp.concatenate([local[0:32, index : index + 1] for index in range(16)], axis=0)
    for copy in copies:
        copy.wait()
    for index in range(4):
        part = slice(128 * index, 128 * index + 128)
        picks[part, :] = dot_nn(one_hot(column[part], 0, KEYS), embed[...]).astype(bf16)
    pick_norms = norms_across(picks[...])
    for index in range(2):
        part = slice(512 * index, 512 * index + 512)
        queries = library[part, :]
        near[part, :] = matern(dot_nt(queries * bf16(-2), picks[...]), norms_down(queries), pick_norms)


def between_body(rows_ref, flip_0, flip_1, flip_2, flip_3, picks, local_ref, after, between, query, sems):
    del after
    copies = []
    for index, flip in enumerate((flip_0, flip_1, flip_2, flip_3)):
        copies.append(pltpu.make_async_copy(flip, query.at[index], sems.at[index]))
        copies[-1].start()
    batch, train = places()
    column = jnp.concatenate([local_ref[0:32, index : index + 1] for index in range(8, 16)], axis=0)
    mine = local_rows(rows_ref, train, [batch])[0:1, 0:32]
    mine = jnp.concatenate([mine] * 8, axis=1)
    z = lax.broadcasted_iota(jnp.int32, (256, 256), 1) // 32
    same = jnp.where((column == mine) & (z == train // 4), noise_var / SCALE, 0.0)
    second = picks[256:512, :]
    second_norms = norms_down(second)
    second = second * bf16(-2)
    for index, copy in enumerate(copies):
        copy.wait()
        value = matern(dot_nt(second, query[index]), second_norms, norms_across(query[index]))
        if index == 0:
            value = (value.astype(f32) + same).astype(bf16)
        between[:, 256 * index : 256 * index + 256] = value


def first_body(arrived_ref, own_ref, second_ref, out_ref):
    total = own_ref[0]
    for place in range(32):
        total = total + arrived_ref[place].astype(f32)
    total = total.astype(bf16)
    for place in range(32):
        out_ref[place, 0:16, :] = total
        out_ref[place, 16:32, :] = second_ref[place]


def second_body(arrived_ref, own_ref, between, after, out_ref, resid):
    del after
    batch, train = places()
    total = own_ref[1]
    for place in range(32):
        total = total + arrived_ref[place, 16:32, :].astype(f32)
    own = lax.rem(train, 4)
    for flip in range(4):
        other = lax.bitwise_xor(own, flip)
        for z in range(8):
            start = 256 * flip + 32 * z
            resid[start : start + 32, :] = one_below_other(arrived_ref[4 * z + other, 0:16, :])
    mine = one_below_other(total)
    change = dot_nn(between[...], resid[...]) * (-CUT * SCALE)
    group = lax.broadcasted_iota(jnp.int32, (256, HALF), 0) // 32
    change = change + jnp.where(group == batch, jnp.concatenate([mine] * 8, axis=0), 0.0)
    change = jnp.concatenate([change[0:128], change[128:256]], axis=1).astype(bf16)
    kept = arrived_ref[train, 0:16, :]
    for place in range(8):
        out_ref[place, 0:128, :] = change
        out_ref[place, 128:144, :] = kept


def third_body(arrived_ref, library, near, out_ref, resid_ref):
    second = arrived_ref[0, 0:128, :].astype(f32)
    for place in range(1, 8):
        second = second + arrived_ref[place, 0:128, :].astype(f32)
    second = jnp.concatenate([second[:, 0:HALF], second[:, HALF:]], axis=0)
    first = jnp.concatenate([one_below_other(arrived_ref[place, 128:144, :].astype(f32)) for place in range(8)], axis=0)
    resid_ref[...] = jnp.concatenate([first, second], axis=0)
    resid = jnp.concatenate([CUT * first, step_rate * second], axis=0).astype(bf16)
    total = SCALE * (library[...] - dot_nn(near[...], resid))
    pack(total, out_ref)


def update_body(resid_ref, local_ref, coef_ref, vel_ref, new_coef_ref, new_vel_ref):
    lanes = jnp.concatenate([resid_ref[...], jnp.zeros((512, 128 - HALF), f32)], axis=1)
    across = jnp.transpose(lanes)[0:48]
    grads = []
    for step in range(2):
        column = jnp.concatenate(
            [local_ref[0:32, 8 * step + group : 8 * step + group + 1] for group in range(8)], axis=0
        )
        high, low = two_terms(across[:, 256 * step : 256 * step + 256])
        chosen = one_hot(column, 0, KEYS)
        grads.append((dot_nn(high, chosen) + dot_nn(low, chosen))[0:COLS])
    vel = momentum * vel_ref[...] - step_rate * grads[0]
    coef = coef_ref[...] + vel
    vel = momentum * vel - step_rate * grads[1]
    new_vel_ref[...] = vel
    new_coef_ref[...] = coef + vel


def final_body(arrived_ref, prior_ref, out_ref):
    total = arrived_ref[0].astype(f32)
    for place in range(1, 32):
        total = total + arrived_ref[place].astype(f32)
    total = one_below_other(total)[:, 0:COLS]
    out_ref[...] = total + jnp.concatenate([jnp.zeros((32, 1), f32), jnp.transpose(prior_ref[...])], axis=1)


def exchange(x, axis):
    return lax.all_to_all(x, axis, split_axis=0, concat_axis=0, tiled=True)


def whole(
    batch_rows, train_embed, lib_embed, labels, prior_draws, noise_draws, coefficients, velocity, library_prior
):
    flops = 2 * KEYS * QUERIES * 512
    dma = pltpu.SemaphoreType.DMA
    vmem = pltpu.VMEM
    block = ("P", (32, 16, 128), bf16)
    sent, rows = call(
        pick_body, [("H", batch_rows), ("H", train_embed)],
        [("H", (8, 2, 32, 256), bf16), ("V", (2, 8192), jnp.int32)],
        [vmem((KEYS, 256), bf16), vmem((2, 32, 256), bf16), dma((13,))],
    )
    columns = [[4 * z + chip for z in range(8)] for chip in range(4)]
    column = lax.all_to_all(sent, "train", 0, 0, axis_index_groups=columns, tiled=True)
    flips = []
    for step in range(2):
        own_part = column[:, step].reshape(256, 256)
        flips.append([own_part])
        for flip in range(1, 4):
            flips[step].append(lax.ppermute(own_part, "train", [(t, t ^ flip) for t in range(32)]))
    state = vmem((COLS, KEYS), f32)
    draws = vmem((COLS - 1, KEYS), f32)
    half = vmem((HALF, KEYS), bf16)
    ahead, base, own, norms = call(
        prep_body,
        [
            ("V", rows), ("H", train_embed), ("H", labels[None, :]), ("H", prior_draws),
            ("H", noise_draws), ("H", coefficients), ("H", velocity),
        ],
        [
            ("H", (HALF, KEYS), bf16), ("H", (HALF, KEYS), bf16), ("V", (2, 16, 128), f32), ("V", (1, KEYS), f32),
        ],
        [vmem((KEYS, 256), bf16), vmem((1, KEYS), f32), draws, draws, state, state, half, half, dma((8,))],
        flops // 4,
    )
    near, picks, local = call(
        near_body,
        [("V", rows), ("H", train_embed), ("H", lib_embed), ("H", base)],
        [("V", (QUERIES, 512), bf16), ("V", (512, 256), bf16), ("V", (128, 16), jnp.int32)],
        [vmem((KEYS, 256), bf16), vmem((QUERIES, 256), bf16), dma((2,))], flops // 4,
    )
    library_part = call(
        library_first_body,
        [("H", train_embed), ("H", lib_embed), ("H", base), ("V", norms), ("V", near)],
        [("V", (QUERIES, HALF), f32)], dense_scratch(QUERIES), flops * LIBRARY_SPLIT // 8,
    )
    part_half = call(
        dense_first_body,
        [("H", train_embed), ("A", flips[0][0]), ("A", flips[0][1]), ("H", ahead), ("V", norms), ("V", library_part)],
        [("V", (16, 16, 128), bf16)], dense_scratch(512), flops // 2,
    )
    part_0 = call(
        dense_rest_body,
        [("H", train_embed), ("A", flips[0][2]), ("A", flips[0][3]), ("H", ahead), ("V", norms), ("V", part_half)],
        [block], dense_scratch(512), flops // 2,
    )
    arrived_0 = exchange(part_0, "train")
    part_1 = call(
        dense_second_body,
        [("H", train_embed), *[("A", part) for part in flips[1]], ("H", base), ("V", norms), ("H", part_0)],
        [("V", (32, 16, 128), bf16)], dense_scratch(QUERIES), flops,
    )
    sent_1 = call(first_body, [("V", arrived_0), ("V", own), ("V", part_1)], [("P", (32, 32, 128), bf16)])
    arrived_1 = exchange(sent_1, "train")
    between = call(
        between_body,
        [("V", rows), *[("A", part) for part in flips[0]], ("V", picks), ("V", local), ("H", sent_1)],
        [("V", (256, QUERIES), bf16)], [vmem((4, 256, 256), bf16), dma((4,))], flops // 16,
    )
    library = call(
        library_second_body,
        [("H", train_embed), ("H", lib_embed), ("H", base), ("V", norms), ("V", library_part), ("V", between)],
        [("V", (QUERIES, HALF), f32)], dense_scratch(QUERIES), flops * (8 - LIBRARY_SPLIT) // 8,
    )
    sent_2 = call(
        second_body, [("V", arrived_1), ("V", own), ("V", between), ("V", library)],
        [("V", (8, 144, 128), bf16)], [vmem((QUERIES, HALF), bf16)],
    )
    arrived_2 = exchange(sent_2, "batch")
    sent_3, resid = call(third_body, [("V", arrived_2), ("V", library), ("V", near)], [block, ("V", (512, HALF), f32)])
    arrived_3 = exchange(sent_3, "train")
    new_coef, new_vel = call(
        update_body, [("V", resid), ("V", local), ("V", coefficients), ("V", velocity)],
        [("P", (COLS, KEYS), f32), ("P", (COLS, KEYS), f32)],
    )
    predictions = call(final_body, [("V", arrived_3), ("V", library_prior)], [("P", (32, COLS), f32)])
    return new_coef, new_vel, predictions.T


def solution(mesh):
    return jax.shard_map(
        whole,
        mesh=mesh,
        in_specs=(
            P(),
            P("train", None),
            P("batch", None),
            P("train"),
            P(None, "train"),
            P(None, "train"),
            P(None, "train"),
            P(None, "train"),
            P(None, ("batch", "train")),
        ),
        out_specs=(P(None, "train"), P(None, "train"), P(None, ("batch", "train"))),
        check_vma=False,
    )
```

profile of v0, /device:TPU:1, one launch (start us, length us, event | category | flops | bytes accessed | tf_op | source)
XLA Modules:
  0.0 128.3 jit_solution(4219924418430375940)
XLA Ops:
  0.6 2.9 %shard_map.112 = (bf16[8,2,32,256]{3,2,1,0:T(8,128)(2,1)}, s32[2,8192]{1,0:T(2,128)S(1)}) custom-call(s32[2,8192]{1,0:T(2,128)} %rows_hbm.1, bf16[4096,256]{1,0:T(8,128)(2,1)} %embed.9), custom_call_target="tpu_custom_call" | custom-call | bytes 1048576 | tf_op jit(solution)/shard_map/pallas_call | solution.py:49
  3.6 9.0 %all-to-all-start = ((bf16[8,2,32,256]{3,2,1,0:T(8,128)(2,1)}), bf16[8,2,32,256]{3,2,1,0:T(8,128)(2,1)S(1)}, u32[]{:S(2)}, u32[]{:S(2)}) async-start(bf16[8,2,32,256]{3,2,1,0:T(8,128)(2,1)} %get-tuple-element.16), calls=%async_computation | async-start | bytes 524288 | tf_op jit(solution)/shard_map/all_to_all | solution.py:454
  12.6 4.5 %shard_map.113 = (bf16[64,4096]{1,0:T(8,128)(2,1)}, bf16[64,4096]{1,0:T(8,128)(2,1)}, f32[2,16,128]{2,1,0:T(8,128)S(1)}, f32[1,4096]{1,0:T(1,128)S(1)}) custom-call(s32[2,8192]{1,0:T(2,128)S(1)} %get-tuple-element.17.rows_ref, bf16[4096,256]{1,0:T(8,128)(2,1)} %embed.9, f32[1,4096]{1,0:T(1,128)} %bitcast.13, f32[32,4096]{1,0:T(8,128)} %prior_hbm.1, ...), custom_call_target="tpu_custom_call" | custom-call | flops 1073741824 | bytes 1048576 | tf_op jit(solution)/shard_map/pallas_call | solution.py:49
  17.1 4.3 %shard_map.114 = (bf16[1024,512]{1,0:T(8,128)(2,1)S(1)}, bf16[512,256]{1,0:T(8,128)(2,1)S(1)}, s32[128,16]{1,0:T(8,128)S(1)}) custom-call(s32[2,8192]{1,0:T(2,128)S(1)} %get-tuple-element.17.rows_ref, bf16[4096,256]{1,0:T(8,128)(2,1)} %embed.9, bf16[1024,256]{1,0:T(8,128)(2,1)} %query.3, bf16[64,4096]{1,0:T(8,128)(2,1)} %get-tuple-element.20.after.weight), custom_call_target="tpu_custom_call" | custom-call | flops 1073741824 | bytes 1048576 | tf_op jit(solution)/shard_map/pallas_call | solution.py:49
  21.3 1.7 %all-to-all-done = bf16[8,2,32,256]{3,2,1,0:T(8,128)(2,1)S(1)} async-done(((bf16[8,2,32,256]{3,2,1,0:T(8,128)(2,1)}), bf16[8,2,32,256]{3,2,1,0:T(8,128)(2,1)S(1)}, u32[]{:S(2)}, u32[]{:S(2)}) %all-to-all-start) | async-done | bytes 262176 | tf_op jit(solution)/shard_map/all_to_all | solution.py:454
  23.1 2.4 %collective-permute-start.2 = (bf16[256,256]{1,0:T(8,128)(2,1)S(1)}, bf16[256,256]{1,0:T(8,128)(2,1)S(1)}, u32[]{:S(2)}, u32[]{:S(2)}) collective-permute-start(bf16[256,256]{1,0:T(8,128)(2,1)S(1)} %bitcast.4), channel_id=1, source_target_pairs={{0,1},{1,0},{2,3},{3,2},{4,5},{5,4},{6,7},{7,6},{8,9},{9,8},{10,11... | collective-permute-start | bytes 393224 | tf_op jit(solution)/shard_map/ppermute | solution.py:460
  25.5 6.3 %shard_map.115.after.start_ref = f32[1024,64]{1,0:T(8,128)S(1)} custom-call(bf16[4096,256]{1,0:T(8,128)(2,1)} %embed.9, bf16[1024,256]{1,0:T(8,128)(2,1)} %query.3, bf16[64,4096]{1,0:T(8,128)(2,1)} %get-tuple-element.20.after.weight, f32[1,4096]{1,0:T(1,128)S(1)} %get-tuple-element.19.norms_ref, bf16[1024,512]{1,0:T(8,128)(2,1)S(1)} %get-tuple-element.21.after.near), custom_call_target="tpu_custom_call" | custom-call | flops 2147483648 | bytes 1048576 | tf_op jit(solution)/shard_map/pallas_call | solution.py:49
  31.8 0.0 copy-start.3
  31.8 2.8 %collective-permute-start = (bf16[256,256]{1,0:T(8,128)(2,1)S(1)}, bf16[256,256]{1,0:T(8,128)(2,1)S(1)}, u32[]{:S(2)}, u32[]{:S(2)}) collective-permute-start(bf16[256,256]{1,0:T(8,128)(2,1)S(1)} %bitcast.5), channel_id=1, source_target_pairs={{0,2},{1,3},{2,0},{3,1},{4,6},{5,7},{6,4},{7,5},{8,10},{9,11},{10,... | collective-permute-start | bytes 393224 | tf_op jit(solution)/shard_map/ppermute | solution.py:460
  34.6 0.4 collective-permute-start.1
  35.0 0.2 collective-permute-start.3
  35.3 2.7 %collective-permute-start.4 = (bf16[256,256]{1,0:T(8,128)(2,1)S(1)}, bf16[256,256]{1,0:T(8,128)(2,1)S(1)}, u32[]{:S(2)}, u32[]{:S(2)}) collective-permute-start(bf16[256,256]{1,0:T(8,128)(2,1)S(1)} %bitcast.10), channel_id=1, source_target_pairs={{0,2},{1,3},{2,0},{3,1},{4,6},{5,7},{6,4},{7,5},{8,10},{9,11},{10,... | collective-permute-start | bytes 393224 | tf_op jit(solution)/shard_map/ppermute | solution.py:460
  38.0 0.0 collective-permute-done.2.flip.flip_1
  38.0 0.7 collective-permute-start.5
  38.7 6.5 %shard_map.116.done_ref = bf16[16,16,128]{2,1,0:T(8,128)(2,1)S(1)} custom-call(bf16[4096,256]{1,0:T(8,128)(2,1)} %embed.9, bf16[256,256]{1,0:T(8,128)(2,1)S(1)} %bitcast.7, bf16[256,256]{1,0:T(8,128)(2,1)S(1)} %collective-permute-done.2.flip.flip_1, bf16[64,4096]{1,0:T(8,128)(2,1)} %get-tuple-element.18.weight, f32[1,4096]{1,0:T(1,128)S(1)} %get-tuple-element.19.norms_ref, ...), custom_call_target="tpu_custom_call" | custom-call | flops 2147483648 | bytes 1048576 | tf_op jit(solution)/shard_map/pallas_call | solution.py:49
  45.2 0.0 copy-done.3
  45.2 0.0 collective-permute-done.flip_2
  45.3 0.0 collective-permute-done.1.flip_3
  45.3 7.2 %shard_map.117.after = bf16[32,16,128]{2,1,0:T(8,128)(2,1)} custom-call(bf16[4096,256]{1,0:T(8,128)(2,1)} %embed.9, bf16[256,256]{1,0:T(8,128)(2,1)S(1)} %collective-permute-done.flip_2, bf16[256,256]{1,0:T(8,128)(2,1)S(1)} %collective-permute-done.1.flip_3, bf16[64,4096]{1,0:T(8,128)(2,1)} %get-tuple-element.18.weight, ...), custom_call_target="tpu_custom_call" | custom-call | flops 2147483648 | bytes 1048576 | tf_op jit(solution)/shard_map/pallas_call | solution.py:49
  52.5 6.8 %all-to-all-start.1 = ((bf16[32,16,128]{2,1,0:T(8,128)(2,1)}), bf16[32,16,128]{2,1,0:T(8,128)(2,1)S(1)}, u32[]{:S(2)}, u32[]{:S(2)}) async-start(bf16[32,16,128]{2,1,0:T(8,128)(2,1)} %shard_map.117.after), calls=%async_computation.1 | async-start | bytes 262144 | tf_op jit(solution)/shard_map/all_to_all | solution.py:438
  59.3 0.0 collective-permute-done.3.flip_1
  59.3 0.0 collective-permute-done.4.flip_2
  59.4 0.0 collective-permute-done.5.flip_3
  59.4 11.0 %shard_map.118.second_ref = bf16[32,16,128]{2,1,0:T(8,128)(2,1)S(1)} custom-call(bf16[4096,256]{1,0:T(8,128)(2,1)} %embed.9, bf16[256,256]{1,0:T(8,128)(2,1)S(1)} %bitcast.12, bf16[256,256]{1,0:T(8,128)(2,1)S(1)} %collective-permute-done.3.flip_1, bf16[256,256]{1,0:T(8,128)(2,1)S(1)} %collective-permute-done.4.flip_2, ...), custom_call_target="tpu_custom_call" | custom-call | flops 4294967296 | bytes 1048576 | tf_op jit(solution)/shard_map/pallas_call | solution.py:49
  70.4 0.0 all-to-all-done.1.arrived_ref
  70.4 0.7 shard_map.119.after
  71.2 9.8 %all-to-all-start.2 = ((bf16[32,32,128]{2,1,0:T(8,128)(2,1)}), bf16[32,32,128]{2,1,0:T(8,128)(2,1)}, u32[]{:S(2)}, u32[]{:S(2)}) async-start(bf16[32,32,128]{2,1,0:T(8,128)(2,1)} %shard_map.119.after), calls=%async_computation.2 | async-start | bytes 524288 | tf_op jit(solution)/shard_map/all_to_all | solution.py:438
  81.0 2.8 %shard_map.120.after.between = bf16[256,1024]{1,0:T(8,128)(2,1)S(1)} custom-call(s32[2,8192]{1,0:T(2,128)S(1)} %get-tuple-element.17.rows_ref, bf16[256,256]{1,0:T(8,128)(2,1)S(1)} %bitcast.8, bf16[256,256]{1,0:T(8,128)(2,1)S(1)} %collective-permute-done.2.flip.flip_1, bf16[256,256]{1,0:T(8,128)(2,1)S(1)} %collective-permute-done.flip_2, ...), custom_call_target="tpu_custom_call" | custom-call | flops 268435456 | bytes 1048576 | tf_op jit(solution)/shard_map/pallas_call | solution.py:49
  83.8 0.0 copy-start.4
  83.8 1.0 copy-done.4
  84.8 6.4 %shard_map.121.after.library = f32[1024,64]{1,0:T(8,128)S(1)} custom-call(bf16[4096,256]{1,0:T(8,128)(2,1)} %embed.9, bf16[1024,256]{1,0:T(8,128)(2,1)} %query.3, bf16[64,4096]{1,0:T(8,128)(2,1)} %get-tuple-element.20.after.weight, f32[1,4096]{1,0:T(1,128)S(1)} %get-tuple-element.19.norms_ref, f32[1024,64]{1,0:T(8,128)S(1)} %copy-done.4, ...), custom_call_target="tpu_custom_call" | custom-call | flops 2147483648 | bytes 1048576 | tf_op jit(solution)/shard_map/pallas_call | solution.py:49
  91.2 0.0 copy-start
  91.2 0.0 copy-start.1
  91.2 2.8 %all-to-all-done.2.arrived_ref = bf16[32,32,128]{2,1,0:T(8,128)(2,1)} async-done(((bf16[32,32,128]{2,1,0:T(8,128)(2,1)}), bf16[32,32,128]{2,1,0:T(8,128)(2,1)}, u32[]{:S(2)}, u32[]{:S(2)}) %all-to-all-start.2) | async-done | bytes 262176 | tf_op jit(solution)/shard_map/all_to_all | solution.py:438
  94.0 1.4 %shard_map.122 = bf16[8,144,128]{2,1,0:T(8,128)(2,1)S(1)} custom-call(bf16[32,32,128]{2,1,0:T(8,128)(2,1)} %all-to-all-done.2.arrived_ref, f32[2,16,128]{2,1,0:T(8,128)S(1)} %get-tuple-element.22.own_ref, bf16[256,1024]{1,0:T(8,128)(2,1)S(1)} %shard_map.120.after.between, f32[1024,64]{1,0:T(8,128)S(1)} %shard_map.121.after.library), custom_call_target="tpu_custom_call" | custom-call | bytes 1048576 | tf_op jit(solution)/shard_map/pallas_call | solution.py:49
  95.4 0.0 copy-start.2
  95.4 11.2 %all_to_all.25.arrived_ref = bf16[8,144,128]{2,1,0:T(8,128)(2,1)S(1)} all-to-all(bf16[8,144,128]{2,1,0:T(8,128)(2,1)S(1)} %shard_map.122), channel_id=1, replica_groups=mesh['batch'=8,'train'=32] {'batch'}, dimensions={0} | all-to-all | bytes 589824 | tf_op jit(solution)/shard_map/all_to_all | solution.py:438
  106.6 1.2 shard_map.123
  107.8 8.9 %all-to-all-start.4 = ((bf16[32,16,128]{2,1,0:T(8,128)(2,1)}), bf16[32,16,128]{2,1,0:T(8,128)(2,1)S(1)}, u32[]{:S(2)}, u32[]{:S(2)}) async-start(bf16[32,16,128]{2,1,0:T(8,128)(2,1)} %get-tuple-element.28), calls=%async_computation.4 | async-start | bytes 262144 | tf_op jit(solution)/shard_map/all_to_all | solution.py:438
  116.8 0.0 copy-done
  116.8 0.0 copy-done.1
  116.8 3.4 %shard_map.124 = (f32[33,4096]{1,0:T(8,128)}, f32[33,4096]{1,0:T(8,128)}) custom-call(f32[512,64]{1,0:T(8,128)S(1)} %get-tuple-element.25.resid_ref, s32[128,16]{1,0:T(8,128)S(1)} %get-tuple-element.24.local_ref, f32[33,4096]{1,0:T(8,128)S(1)} %copy-done, f32[33,4096]{1,0:T(8,128)S(1)} %copy-done.1), custom_call_target="tpu_custom_call" | custom-call | bytes 1048576 | tf_op jit(solution)/shard_map/pallas_call | solution.py:49
  120.2 7.3 %all-to-all-done.4.arrived_ref = bf16[32,16,128]{2,1,0:T(8,128)(2,1)S(1)} async-done(((bf16[32,16,128]{2,1,0:T(8,128)(2,1)}), bf16[32,16,128]{2,1,0:T(8,128)(2,1)S(1)}, u32[]{:S(2)}, u32[]{:S(2)}) %all-to-all-start.4) | async-done | bytes 131104 | tf_op jit(solution)/shard_map/all_to_all | solution.py:438
  127.5 0.0 copy-done.2
  127.5 0.8 shard_map.125
  (1 shorter events, 0.0 us)
Async XLA Ops:
  3.6 19.5 %all-to-all-start = ((bf16[8,2,32,256]{3,2,1,0:T(8,128)(2,1)}), bf16[8,2,32,256]{3,2,1,0:T(8,128)(2,1)S(1)}, u32[]{:S(2)}, u32[]{:S(2)}) async-start(bf16[8,2,32,256]{3,2,1,0:T(8,128)(2,1)} %get-tuple-element.16), calls=%async_computation | async-start | bytes 524288 | tf_op jit(solution)/shard_map/all_to_all | solution.py:454
  23.1 14.9 %collective-permute-start.2 = (bf16[256,256]{1,0:T(8,128)(2,1)S(1)}, bf16[256,256]{1,0:T(8,128)(2,1)S(1)}, u32[]{:S(2)}, u32[]{:S(2)}) collective-permute-start(bf16[256,256]{1,0:T(8,128)(2,1)S(1)} %bitcast.4), channel_id=1, source_target_pairs={{0,1},{1,0},{2,3},{3,2},{4,5},{5,4},{6,7},{7,6},{8,9},{9,8},{10,11... | collective-permute-start | bytes 393224 | tf_op jit(solution)/shard_map/ppermute | solution.py:460
  31.8 13.4 %copy-start.3 = (f32[1024,64]{1,0:T(8,128)}, f32[1024,64]{1,0:T(8,128)S(1)}, u32[]{:S(2)}) copy-start(f32[1024,64]{1,0:T(8,128)S(1)} %shard_map.115.after.start_ref) | copy-start | bytes 786436
  31.8 13.4 %collective-permute-start = (bf16[256,256]{1,0:T(8,128)(2,1)S(1)}, bf16[256,256]{1,0:T(8,128)(2,1)S(1)}, u32[]{:S(2)}, u32[]{:S(2)}) collective-permute-start(bf16[256,256]{1,0:T(8,128)(2,1)S(1)} %bitcast.5), channel_id=1, source_target_pairs={{0,2},{1,3},{2,0},{3,1},{4,6},{5,7},{6,4},{7,5},{8,10},{9,11},{10,... | collective-permute-start | bytes 393224 | tf_op jit(solution)/shard_map/ppermute | solution.py:460
  34.6 10.6 %collective-permute-start.1 = (bf16[256,256]{1,0:T(8,128)(2,1)S(1)}, bf16[256,256]{1,0:T(8,128)(2,1)S(1)}, u32[]{:S(2)}, u32[]{:S(2)}) collective-permute-start(bf16[256,256]{1,0:T(8,128)(2,1)S(1)} %bitcast.6), channel_id=1, source_target_pairs={{0,3},{1,2},{2,1},{3,0},{4,7},{5,6},{6,5},{7,4},{8,11},{9,10},{10,... | collective-permute-start | bytes 393224 | tf_op jit(solution)/shard_map/ppermute | solution.py:460
  35.0 24.3 %collective-permute-start.3 = (bf16[256,256]{1,0:T(8,128)(2,1)S(1)}, bf16[256,256]{1,0:T(8,128)(2,1)S(1)}, u32[]{:S(2)}, u32[]{:S(2)}) collective-permute-start(bf16[256,256]{1,0:T(8,128)(2,1)S(1)} %bitcast.9), channel_id=1, source_target_pairs={{0,1},{1,0},{2,3},{3,2},{4,5},{5,4},{6,7},{7,6},{8,9},{9,8},{10,11... | collective-permute-start | bytes 393224 | tf_op jit(solution)/shard_map/ppermute | solution.py:460
  35.3 24.1 %collective-permute-start.4 = (bf16[256,256]{1,0:T(8,128)(2,1)S(1)}, bf16[256,256]{1,0:T(8,128)(2,1)S(1)}, u32[]{:S(2)}, u32[]{:S(2)}) collective-permute-start(bf16[256,256]{1,0:T(8,128)(2,1)S(1)} %bitcast.10), channel_id=1, source_target_pairs={{0,2},{1,3},{2,0},{3,1},{4,6},{5,7},{6,4},{7,5},{8,10},{9,11},{10,... | collective-permute-start | bytes 393224 | tf_op jit(solution)/shard_map/ppermute | solution.py:460
  38.0 21.4 %collective-permute-start.5 = (bf16[256,256]{1,0:T(8,128)(2,1)S(1)}, bf16[256,256]{1,0:T(8,128)(2,1)S(1)}, u32[]{:S(2)}, u32[]{:S(2)}) collective-permute-start(bf16[256,256]{1,0:T(8,128)(2,1)S(1)} %bitcast.11), channel_id=1, source_target_pairs={{0,3},{1,2},{2,1},{3,0},{4,7},{5,6},{6,5},{7,4},{8,11},{9,10},{10,... | collective-permute-start | bytes 393224 | tf_op jit(solution)/shard_map/ppermute | solution.py:460
  52.5 17.9 %all-to-all-start.1 = ((bf16[32,16,128]{2,1,0:T(8,128)(2,1)}), bf16[32,16,128]{2,1,0:T(8,128)(2,1)S(1)}, u32[]{:S(2)}, u32[]{:S(2)}) async-start(bf16[32,16,128]{2,1,0:T(8,128)(2,1)} %shard_map.117.after), calls=%async_computation.1 | async-start | bytes 262144 | tf_op jit(solution)/shard_map/all_to_all | solution.py:438
  71.2 22.8 %all-to-all-start.2 = ((bf16[32,32,128]{2,1,0:T(8,128)(2,1)}), bf16[32,32,128]{2,1,0:T(8,128)(2,1)}, u32[]{:S(2)}, u32[]{:S(2)}) async-start(bf16[32,32,128]{2,1,0:T(8,128)(2,1)} %shard_map.119.after), calls=%async_computation.2 | async-start | bytes 524288 | tf_op jit(solution)/shard_map/all_to_all | solution.py:438
  83.8 1.0 copy-start.4
  91.2 25.6 %copy-start = (f32[33,4096]{1,0:T(8,128)S(1)}, f32[33,4096]{1,0:T(8,128)}, u32[]{:S(2)}) copy-start(f32[33,4096]{1,0:T(8,128)} %coef_ref.1) | copy-start | bytes 1622020
  91.2 25.6 %copy-start.1 = (f32[33,4096]{1,0:T(8,128)S(1)}, f32[33,4096]{1,0:T(8,128)}, u32[]{:S(2)}) copy-start(f32[33,4096]{1,0:T(8,128)} %vel_ref.1) | copy-start | bytes 1622020
  95.4 32.1 %copy-start.2 = (f32[32,32]{1,0:T(8,128)S(1)}, f32[32,32]{1,0:T(8,128)}, u32[]{:S(2)}) copy-start(f32[32,32]{1,0:T(8,128)} %prior_ref.1) | copy-start | bytes 12292
  107.8 19.7 %all-to-all-start.4 = ((bf16[32,16,128]{2,1,0:T(8,128)(2,1)}), bf16[32,16,128]{2,1,0:T(8,128)(2,1)S(1)}, u32[]{:S(2)}, u32[]{:S(2)}) async-start(bf16[32,16,128]{2,1,0:T(8,128)(2,1)} %get-tuple-element.28), calls=%async_computation.4 | async-start | bytes 262144 | tf_op jit(solution)/shard_map/all_to_all | solution.py:438
where the time goes:
time: 129 us; the launch traced here: 128 us
  Pallas kernels  59.3 us (46%)
  starting transfers between devices  43.9 us (34%)
  waiting for transfers between devices  11.9 us (9%)
  blocking collectives  11.2 us (9%)
    pallas_call x14, Pallas kernels, call(): kernel(*[pltpu.with_memory_space_constraint(array, space[kind]) for kind,...  59.3 us
    all_to_all x3, starting transfers between devices, exchange(): return lax.all_to_all(x, axis, split_axis=0, concat_axis=0, tiled=True)  25.6 us
    all_to_all x1, blocking collectives, exchange(): return lax.all_to_all(x, axis, split_axis=0, concat_axis=0, tiled=True)  11.2 us
    all_to_all x3, waiting for transfers between devices, exchange(): return lax.all_to_all(x, axis, split_axis=0, concat_axis=0, tiled=True)  10.1 us
    ppermute x6, starting transfers between devices, whole(): lax.ppermute(own_part, 'train', [(t, t ^ flip) for t in range(32)])  9.32 us
    all_to_all x1, starting transfers between devices, whole(): lax.all_to_all(sent, 'train', 0, 0, axis_index_groups=columns, tiled=True)  9.02 us
  transfers between devices with their start and end apart: 10, of which 3 were waited for; matrix products, arithmetic and copies ran while one was open for 0% of the time, Pallas kernels for 41%

commit v1 on v0

--- a/solution.py
+++ b/solution.py
@@ -120,7 +120,7 @@
         other = lax.bitwise_xor(own, flip)
         for z in range(8):
             start = 256 * index + 32 * z
-            out_ref[4 * z + other] = (SCALE * side_by_side(total[start : start + 32])).astype(bf16)
+            out_ref[4 * z + other] = (SCALE * side_by_side(total[start : start + 32, 0:HALF])).astype(bf16)
 
 
 def pick_body(rows_hbm, embed_hbm, sent_hbm, rows, embed, picked, sems):
@@ -149,34 +149,46 @@
         copy.wait()
 
 
+def turned(state):
+    full = jnp.concatenate([state, jnp.zeros((40 - COLS, KEYS), f32)], axis=0)
+    rest = jnp.zeros((128, 128 - 40), f32)
+    return [
+        jnp.concatenate([jnp.transpose(full[:, 128 * index : 128 * index + 128]), rest], axis=1).astype(bf16)
+        for index in range(KEYS // 128)
+    ]
+
+
 def prep_body(
-    rows_ref, embed_hbm, labels_hbm, prior_hbm, noise_hbm, coef_hbm, vel_hbm,
-    ahead_hbm, base_hbm, own_ref, norms_ref,
-    embed, labels, prior, noise, coef, vel, ahead_half, base_half, sems,
+    rows_ref, embed_hbm, library_hbm, labels_hbm, prior_hbm, noise_hbm, coef_hbm, vel_hbm,
+    ahead_hbm, base_hbm, own_ref, norms_ref, picks, local_ref, part_hbm,
+    labels, prior, noise, coef, vel, ahead_half, sems, *scratch,
 ):
+    embed, query, base_half, query_norms, cross, total, _ = scratch
     batch, train = places()
     copies = [
         pltpu.make_async_copy(source, target, sems.at[index])
         for index, (source, target) in enumerate(
             [
                 (coef_hbm, coef), (vel_hbm, vel), (prior_hbm, prior), (noise_hbm, noise), (labels_hbm, labels),
-                (embed_hbm, embed),
+                (embed_hbm, embed), (library_hbm, query),
             ]
         )
     ]
     for copy in copies:
         copy.start()
     mine = jnp.transpose(local_rows(rows_ref, train, [batch]))
+    local = jnp.transpose(local_rows(rows_ref, train, range(8)))
+    local_ref[...] = local
     for copy in copies[:2]:
         copy.wait()
     ahead = coef[...] + momentum * vel[...]
     base = coef[...] + CARRY * vel[...]
-    pad = jnp.zeros((HALF - COLS, KEYS), f32)
-    ahead_half[...] = jnp.concatenate([ahead, pad], axis=0).astype(bf16)
-    base_half[...] = jnp.concatenate([base, pad], axis=0).astype(bf16)
+    for index, (one, two) in enumerate(zip(turned(ahead), turned(base))):
+        ahead_half[128 * index : 128 * index + 128, :] = one
+        base_half[128 * index : 128 * index + 128, :] = two
     out = [
-        pltpu.make_async_copy(ahead_half, ahead_hbm, sems.at[6]),
-        pltpu.make_async_copy(base_half, base_hbm, sems.at[7]),
+        pltpu.make_async_copy(ahead_half, ahead_hbm, sems.at[7]),
+        pltpu.make_async_copy(base_half, base_hbm, sems.at[8]),
     ]
     for copy in out:
         copy.start()
@@ -184,104 +196,129 @@
         copy.wait()
     shift = jnp.concatenate([jnp.zeros((1, KEYS), f32), prior[...] + noise_scale * noise[...]], axis=0)
     targets = labels[...] - shift
+    pad = jnp.zeros((HALF - COLS, KEYS), f32)
     for step, state in enumerate((ahead, base)):
         chosen = one_hot(mine[0:32, step : step + 1], 0, KEYS)
         high, low = two_terms(jnp.concatenate([noise_var * state - targets, pad], axis=0))
         own_ref[step] = side_by_side(dot_nt(chosen, high) + dot_nt(chosen, low))
     norms_ref[...] = norms_across(embed[...])
+    column = jnp.concatenate([local[0:32, index : index + 1] for index in range(16)], axis=0)
+    for index in range(4):
+        part = slice(128 * index, 128 * index + 128)
+        picks[part, :] = dot_nn(one_hot(column[part], 0, KEYS), embed[...]).astype(bf16)
+    total[...] = jnp.zeros_like(total)
+    scaled(query, query_norms, slice(0, QUERIES))
+    sweep(embed, query, base_half, query_norms, cross, total, norms_ref, (0, LIBRARY_SPLIT), None, True)
+    out.append(pltpu.make_async_copy(total, part_hbm, sems.at[9]))
+    out[-1].start()
     for copy in out:
         copy.wait()
+
+
+LIBRARY_SPLIT = 4
+
+
+def scaled(query, query_norms, part):
+    query_norms[part, :] = norms_down(query[part, :])
+    query[part, :] = query[part, :] * bf16(-2)
+
+
+def sweep(embed, query, weight, query_norms, cross, total, norms_ref, tiles, wait, short):
+    first, count = tiles
+
+    def keys(index):
+        return pl.ds(pl.multiple_of((first + index) * TILE, TILE), TILE)
+
+    def product(index):
+        return dot_nt(query[...], embed[keys(index), :])
+
+    def one(index, slot, more):
+        if more:
+            cross[1 - slot] = product(jnp.minimum(index + 1, count - 1) if short else index + 1)
+        value = matern(cross[slot], query_norms[...], norms_ref[:, keys(index)])
+        total[...] += dot_nn(value, weight[keys(index), :])
+
+    if wait is not None:
+        wait(0)
+    cross[0] = product(0)
+
+    def pair(index, carry):
+        if wait is not None:
+            wait(2 * index + 1)
+            if short:
+                pl.when(2 * index + 2 < count)(lambda: wait(2 * index + 2))
+            else:
+                wait(2 * index + 2)
+        one(2 * index, 0, True)
+        one(2 * index + 1, 1, True)
+        return carry
+
+    loops = count // 2 if short else (count - 1) // 2
+    lax.fori_loop(0, loops, pair, 0)
+    for index in range(2 * loops, count):
+        more = index + 1 < count
+        if more and wait is not None:
+            wait(index + 1)
+        one(index, index % 2, more)
 
 
 def dense_scratch(queries):
     return [
         pltpu.VMEM((KEYS, 256), bf16),
         pltpu.VMEM((queries, 256), bf16),
-        pltpu.VMEM((HALF, KEYS), bf16),
+        pltpu.VMEM((KEYS, 128), bf16),
         pltpu.VMEM((queries, 1), f32),
         pltpu.VMEM((2, queries, TILE), f32),
-        pltpu.VMEM((queries, HALF), f32),
-        pltpu.SemaphoreType.DMA((13,)),
+        pltpu.VMEM((queries, 128), f32),
+        pltpu.SemaphoreType.DMA((20,)),
     ]
 
 
-def dense(embed_hbm, pieces, weight_hbm, norms_ref, scratch, tiles, start_ref=None, short=False):
-    embed, query, weight, query_norms, cross, total_ref, sems = scratch
+def dense(embed_hbm, pieces, weight_hbm, norms_ref, scratch, tiles, start_hbm=None, between=None, short=False):
+    embed, query, weight, query_norms, cross, total, sems = scratch
     first, count = tiles
 
     def chunk(index):
         part = pl.ds(pl.multiple_of((first + index) * TILE, TILE), TILE)
-        return pltpu.make_async_copy(embed_hbm.at[part], embed.at[part], sems.at[index])
+        return (
+            pltpu.make_async_copy(embed_hbm.at[part], embed.at[part], sems.at[index]),
+            pltpu.make_async_copy(weight_hbm.at[part], weight.at[part], sems.at[8 + index]),
+        )
+
+    def wait(index):
+        for copy in chunk(index):
+            copy.wait()
 
     rows = query.shape[0] // len(pieces)
     fetches = [
-        pltpu.make_async_copy(piece, query.at[pl.ds(rows * index, rows)], sems.at[9 + index])
+        pltpu.make_async_copy(piece, query.at[pl.ds(rows * index, rows)], sems.at[16 + index])
         for index, piece in enumerate(pieces)
     ]
-    fetch_weight = pltpu.make_async_copy(weight_hbm, weight, sems.at[8])
     for fetch in fetches:
         fetch.start()
-    chunk(0).start()
-    fetch_weight.start()
-    for index in range(1, count):
-        chunk(index).start()
-    total_ref[...] = jnp.zeros_like(total_ref) if start_ref is None else start_ref[...]
+    for index in range(count):
+        for copy in chunk(index):
+            copy.start()
+    if start_hbm is None:
+        total[...] = jnp.zeros_like(total)
+    else:
+        fetch_start = pltpu.make_async_copy(start_hbm, total, sems.at[17])
+        fetch_start.start()
+    if between is not None:
+        between()
     for index, fetch in enumerate(fetches):
         fetch.wait()
-        part = slice(rows * index, rows * index + rows)
-        query_norms[part, :] = norms_down(query[part, :])
-        query[part, :] = query[part, :] * bf16(-2)
-
-    def keys(index):
-        return pl.ds(pl.multiple_of((first + index) * TILE, TILE), TILE)
-
-    def product(index):
-        return dot_nt(query[...], embed[keys(index), :])
-
-    chunk(0).wait()
-    cross[0] = product(0)
-    fetch_weight.wait()
-
-    def one(index, slot, more):
-        if more:
-            cross[1 - slot] = product(jnp.minimum(index + 1, count - 1) if short else index + 1)
-        value = matern(cross[slot], query_norms[...], norms_ref[:, keys(index)])
-        total_ref[...] += dot_nt(value, weight[:, keys(index)])
-
-    def pair(index, carry):
-        chunk(2 * index + 1).wait()
-        if short:
-
-            @pl.when(2 * index + 2 < count)
-            def _():
-                chunk(2 * index + 2).wait()
-
-            one(2 * index, 0, True)
-            one(2 * index + 1, 1, True)
-        else:
-            chunk(2 * index + 2).wait()
-            one(2 * index, 0, True)
-            one(2 * index + 1, 1, True)
-        return carry
-
-    if short:
-        lax.fori_loop(0, count // 2, pair, 0)
-        return total_ref
-    loops = (count - 1) // 2
-    lax.fori_loop(0, loops, pair, 0)
-    for index in range(2 * loops, count):
-        more = index + 1 < count
-        if more:
-            chunk(index + 1).wait()
-        one(index, index % 2, more)
-    return total_ref
-
-
-def dense_first_body(embed, own, flip, weight, norms_ref, after, out_ref, *scratch):
-    del after
+        scaled(query, query_norms, slice(rows * index, rows * index + rows))
+    if start_hbm is not None:
+        fetch_start.wait()
+    sweep(embed, query, weight, query_norms, cross, total, norms_ref, tiles, wait, short)
+    return total
+
+
+def dense_first_body(embed, own, flip, weight, norms_ref, out_ref, *scratch):
     total = dense(embed, [own, flip], weight, norms_ref, scratch, (0, 8))
     for index in range(16):
-        out_ref[index] = (SCALE * side_by_side(total[32 * index : 32 * index + 32])).astype(bf16)
+        out_ref[index] = (SCALE * side_by_side(total[32 * index : 32 * index + 32, 0:HALF])).astype(bf16)
 
 
 def dense_rest_body(embed, flip_2, flip_3, weight, norms_ref, done_ref, out_ref, *scratch):
@@ -301,66 +338,48 @@
     pack_flipped(total, places()[1], range(4), out_ref)
 
 
-LIBRARY_SPLIT = 4
-
-
-def library_first_body(embed, query, weight, norms_ref, after, out_ref, *scratch):
+def between_body(
+    rows_ref, flip_0, flip_1, flip_2, flip_3, picks, local_ref, embed_hbm, library_hbm, weight_hbm, norms_ref, start_hbm,
+    after, between, out_ref, first, sems, *scratch,
+):
     del after
-    total = dense(embed, [query], weight, norms_ref, scratch, (0, LIBRARY_SPLIT), short=True)
+    copies = []
+    for index, flip in enumerate((flip_0, flip_1, flip_2, flip_3)):
+        copies.append(pltpu.make_async_copy(flip, first.at[index], sems.at[index]))
+        copies[-1].start()
+
+    def tile():
+        batch, train = places()
+        column = jnp.concatenate([local_ref[0:32, index : index + 1] for index in range(8, 16)], axis=0)
+        mine = local_rows(rows_ref, train, [batch])[0:1, 0:32]
+        mine = jnp.concatenate([mine] * 8, axis=1)
+        z = lax.broadcasted_iota(jnp.int32, (256, 256), 1) // 32
+        same = jnp.where((column == mine) & (z == train // 4), noise_var / SCALE, 0.0)
+        second = picks[256:512, :]
+        second_norms = norms_down(second)
+        second = second * bf16(-2)
+        for index, copy in enumerate(copies):
+            copy.wait()
+            value = matern(dot_nt(second, first[index]), second_norms, norms_across(first[index]))
+            if index == 0:
+                value = (value.astype(f32) + same).astype(bf16)
+            between[:, 256 * index : 256 * index + 256] = value
+
+    tiles = (LIBRARY_SPLIT, 8 - LIBRARY_SPLIT)
+    total = dense(embed_hbm, [library_hbm], weight_hbm, norms_ref, scratch, tiles, start_hbm, tile, True)
     out_ref[...] = total[...]
 
 
-def library_second_body(embed, query, weight, norms_ref, start_ref, after, out_ref, *scratch):
+def near_body(library_hbm, picks, after, near, library, sem):
     del after
-    total = dense(embed, [query], weight, norms_ref, scratch, (LIBRARY_SPLIT, 8 - LIBRARY_SPLIT), start_ref, True)
-    out_ref[...] = total[...]
-
-
-def near_body(rows_ref, embed_hbm, library_hbm, after, near, picks, local_ref, embed, library, sems):
-    del after
-    copies = [
-        pltpu.make_async_copy(embed_hbm, embed, sems.at[0]),
-        pltpu.make_async_copy(library_hbm, library, sems.at[1]),
-    ]
-    for copy in copies:
-        copy.start()
-    train = places()[1]
-    local = jnp.transpose(local_rows(rows_ref, train, range(8)))
-    local_ref[...] = local
-    column = jnp.concatenate([local[0:32, index : index + 1] for index in range(16)], axis=0)
-    for copy in copies:
-        copy.wait()
-    for index in range(4):
-        part = slice(128 * index, 128 * index + 128)
-        picks[part, :] = dot_nn(one_hot(column[part], 0, KEYS), embed[...]).astype(bf16)
+    copy = pltpu.make_async_copy(library_hbm, library, sem)
+    copy.start()
     pick_norms = norms_across(picks[...])
+    copy.wait()
     for index in range(2):
         part = slice(512 * index, 512 * index + 512)
         queries = library[part, :]
         near[part, :] = matern(dot_nt(queries * bf16(-2), picks[...]), norms_down(queries), pick_norms)
-
-
-def between_body(rows_ref, flip_0, flip_1, flip_2, flip_3, picks, local_ref, after, between, query, sems):
-    del after
-    copies = []
-    for index, flip in enumerate((flip_0, flip_1, flip_2, flip_3)):
-        copies.append(pltpu.make_async_copy(flip, query.at[index], sems.at[index]))
-        copies[-1].start()
-    batch, train = places()
-    column = jnp.concatenate([local_ref[0:32, index : index + 1] for index in range(8, 16)], axis=0)
-    mine = local_rows(rows_ref, train, [batch])[0:1, 0:32]
-    mine = jnp.concatenate([mine] * 8, axis=1)
-    z = lax.broadcasted_iota(jnp.int32, (256, 256), 1) // 32
-    same = jnp.where((column == mine) & (z == train // 4), noise_var / SCALE, 0.0)
-    second = picks[256:512, :]
-    second_norms = norms_down(second)
-    second = second * bf16(-2)
-    for index, copy in enumerate(copies):
-        copy.wait()
-        value = matern(dot_nt(second, query[index]), second_norms, norms_across(query[index]))
-        if index == 0:
-            value = (value.astype(f32) + same).astype(bf16)
-        between[:, 256 * index : 256 * index + 256] = value
 
 
 def first_body(arrived_ref, own_ref, second_ref, out_ref):
@@ -373,8 +392,7 @@
         out_ref[place, 16:32, :] = second_ref[place]
 
 
-def second_body(arrived_ref, own_ref, between, after, out_ref, resid):
-    del after
+def second_body(arrived_ref, own_ref, between, out_ref, resid):
     batch, train = places()
     total = own_ref[1]
     for place in range(32):
@@ -404,7 +422,7 @@
     first = jnp.concatenate([one_below_other(arrived_ref[place, 128:144, :].astype(f32)) for place in range(8)], axis=0)
     resid_ref[...] = jnp.concatenate([first, second], axis=0)
     resid = jnp.concatenate([CUT * first, step_rate * second], axis=0).astype(bf16)
-    total = SCALE * (library[...] - dot_nn(near[...], resid))
+    total = SCALE * (library[:, 0:HALF] - dot_nn(near[...], resid))
     pack(total, out_ref)
 
 
@@ -460,33 +478,27 @@
             flips[step].append(lax.ppermute(own_part, "train", [(t, t ^ flip) for t in range(32)]))
     state = vmem((COLS, KEYS), f32)
     draws = vmem((COLS - 1, KEYS), f32)
-    half = vmem((HALF, KEYS), bf16)
-    ahead, base, own, norms = call(
+    turned_state = ("H", (KEYS, 128), bf16)
+    library_total = (QUERIES, 128)
+    ahead, base, own, norms, picks, local, library_part = call(
         prep_body,
         [
-            ("V", rows), ("H", train_embed), ("H", labels[None, :]), ("H", prior_draws),
+            ("V", rows), ("H", train_embed), ("H", lib_embed), ("H", labels[None, :]), ("H", prior_draws),
             ("H", noise_draws), ("H", coefficients), ("H", velocity),
         ],
         [
-            ("H", (HALF, KEYS), bf16), ("H", (HALF, KEYS), bf16), ("V", (2, 16, 128), f32), ("V", (1, KEYS), f32),
+            turned_state, turned_state, ("V", (2, 16, 128), f32), ("V", (1, KEYS), f32), ("V", (512, 256), bf16),
+            ("V", (128, 16), jnp.int32), ("H", library_total, f32),
         ],
-        [vmem((KEYS, 256), bf16), vmem((1, KEYS), f32), draws, draws, state, state, half, half, dma((8,))],
-        flops // 4,
-    )
-    near, picks, local = call(
-        near_body,
-        [("V", rows), ("H", train_embed), ("H", lib_embed), ("H", base)],
-        [("V", (QUERIES, 512), bf16), ("V", (512, 256), bf16), ("V", (128, 16), jnp.int32)],
-        [vmem((KEYS, 256), bf16), vmem((QUERIES, 256), bf16), dma((2,))], flops // 4,
-    )
-    library_part = call(
-        library_first_body,
-        [("H", train_embed), ("H", lib_embed), ("H", base), ("V", norms), ("V", near)],
-        [("V", (QUERIES, HALF), f32)], dense_scratch(QUERIES), flops * LIBRARY_SPLIT // 8,
+        [
+            vmem((1, KEYS), f32), draws, draws, state, state, vmem((KEYS, 128), bf16), dma((10,)),
+            *dense_scratch(QUERIES),
+        ],
+        flops,
     )
     part_half = call(
         dense_first_body,
-        [("H", train_embed), ("A", flips[0][0]), ("A", flips[0][1]), ("H", ahead), ("V", norms), ("V", library_part)],
+        [("H", train_embed), ("A", flips[0][0]), ("A", flips[0][1]), ("H", ahead), ("V", norms)],
         [("V", (16, 16, 128), bf16)], dense_scratch(512), flops // 2,
     )
     part_0 = call(
@@ -502,19 +514,22 @@
     )
     sent_1 = call(first_body, [("V", arrived_0), ("V", own), ("V", part_1)], [("P", (32, 32, 128), bf16)])
     arrived_1 = exchange(sent_1, "train")
-    between = call(
+    between, library = call(
         between_body,
-        [("V", rows), *[("A", part) for part in flips[0]], ("V", picks), ("V", local), ("H", sent_1)],
-        [("V", (256, QUERIES), bf16)], [vmem((4, 256, 256), bf16), dma((4,))], flops // 16,
-    )
-    library = call(
-        library_second_body,
-        [("H", train_embed), ("H", lib_embed), ("H", base), ("V", norms), ("V", library_part), ("V", between)],
-        [("V", (QUERIES, HALF), f32)], dense_scratch(QUERIES), flops * (8 - LIBRARY_SPLIT) // 8,
+        [
+            ("V", rows), *[("A", part) for part in flips[0]], ("V", picks), ("V", local), ("H", train_embed),
+            ("H", lib_embed), ("H", base), ("V", norms), ("H", library_part), ("H", sent_1),
+        ],
+        [("V", (256, QUERIES), bf16), ("V", library_total, f32)],
+        [vmem((4, 256, 256), bf16), dma((4,)), *dense_scratch(QUERIES)], flops // 2,
     )
     sent_2 = call(
-        second_body, [("V", arrived_1), ("V", own), ("V", between), ("V", library)],
-        [("V", (8, 144, 128), bf16)], [vmem((QUERIES, HALF), bf16)],
+        second_body, [("V", arrived_1), ("V", own), ("V", between)],
+        [("P", (8, 144, 128), bf16)], [vmem((QUERIES, HALF), bf16)],
+    )
+    near = call(
+        near_body, [("H", lib_embed), ("V", picks), ("H", sent_2)],
+        [("V", (QUERIES, 512), bf16)], [vmem((QUERIES, 256), bf16), dma], flops // 8,
     )
     arrived_2 = exchange(sent_2, "batch")
     sent_3, resid = call(third_body, [("V", arrived_2), ("V", library), ("V", near)], [block, ("V", (512, HALF), f32)])

time: 129 us -> 127 us (0.984)
  starting transfers between devices: 43.9 us -> 33.8 us
  blocking collectives: 11.2 us -> 19.5 us
  waiting for transfers between devices: 11.9 us -> 17.8 us
  Pallas kernels: 59.3 us -> 54.3 us
    all_to_all x1 -> x0, starting transfers between devices: 9.02 us -> none  [whole(): lax.all_to_all(sent, 'train', 0, 0, axis_index_groups=columns, tiled=True)]
    all_to_all x1, blocking collectives: 11.2 us -> 19.5 us  [whole(): lax.all_to_all(sent, 'train', 0, 0, axis_index_groups=columns, tiled=True)]
    all_to_all x3 -> x4, waiting for transfers between devices: 10.1 us -> 17.8 us  [exchange(): return lax.all_to_all(x, axis, split_axis=0, concat_axis=0, tiled=True)]
    pallas_call x14 -> x12, Pallas kernels: 59.3 us -> 54.3 us  [call(): kernel(*[pltpu.with_memory_space_constraint(array, space[kind]) for kind,...]
    all_to_all x1 -> x0, waiting for transfers between devices: 1.74 us -> none  [whole(): lax.all_to_all(sent, 'train', 0, 0, axis_index_groups=columns, tiled=True)]
    all_to_all x3 -> x4, starting transfers between devices: 25.6 us -> 24.5 us  [exchange(): return lax.all_to_all(x, axis, split_axis=0, concat_axis=0, tiled=True)]
  transfers between devices with their start and end apart: 10 -> 10, of which waited for: 3 -> 4; matrix products, arithmetic and copies ran while one was open for 0% -> 0% of each run, Pallas kernels for 41% -> 38%
where the time goes in v1:
time: 127 us; the launch traced here: 126 us
  Pallas kernels  54.3 us (43%)
  starting transfers between devices  33.8 us (27%)
  blocking collectives  19.5 us (15%)
  waiting for transfers between devices  17.8 us (14%)
    pallas_call x12, Pallas kernels, call(): kernel(*[pltpu.with_memory_space_constraint(array, space[kind]) for kind,...  54.3 us
    all_to_all x4, starting transfers between devices, exchange(): return lax.all_to_all(x, axis, split_axis=0, concat_axis=0, tiled=True)  24.5 us
    all_to_all x1, blocking collectives, whole(): lax.all_to_all(sent, 'train', 0, 0, axis_index_groups=columns, tiled=True)  19.5 us
    all_to_all x4, waiting for transfers between devices, exchange(): return lax.all_to_all(x, axis, split_axis=0, concat_axis=0, tiled=True)  17.8 us
    ppermute x6, starting transfers between devices, whole(): lax.ppermute(own_part, 'train', [(t, t ^ flip) for t in range(32)])  9.34 us
  transfers between devices with their start and end apart: 10, of which 4 were waited for; matrix products, arithmetic and copies ran while one was open for 0% of the time, Pallas kernels for 38%

profile of v1, /device:TPU:1, one launch (start us, length us, event | category | flops | bytes accessed | tf_op | source)
XLA Modules:
  0.0 126.2 jit_solution(5915658110757032016)
XLA Ops:
  0.6 2.9 %shard_map.112 = (bf16[8,2,32,256]{3,2,1,0:T(8,128)(2,1)}, s32[2,8192]{1,0:T(2,128)S(1)}) custom-call(s32[2,8192]{1,0:T(2,128)} %rows_hbm.1, bf16[4096,256]{1,0:T(8,128)(2,1)} %embed_hbm.5), custom_call_target="tpu_custom_call" | custom-call | bytes 1048576 | tf_op jit(solution)/shard_map/pallas_call | solution.py:49
  3.6 19.5 %all_to_all.25 = bf16[8,2,32,256]{3,2,1,0:T(8,128)(2,1)S(1)} all-to-all(bf16[8,2,32,256]{3,2,1,0:T(8,128)(2,1)} %get-tuple-element.18), channel_id=1, replica_groups={{0,4,8,12,16,20,24,28},{1,5,9,13,17,21,25,29},{2,6,10,14,18,22,26,30},{..., dimensions={0} | all-to-all | bytes 524288 | tf_op jit(solution)/shard_map/all_to_all | solution.py:472
  23.1 2.4 %collective-permute-start.2 = (bf16[256,256]{1,0:T(8,128)(2,1)S(1)}, bf16[256,256]{1,0:T(8,128)(2,1)S(1)}, u32[]{:S(2)}, u32[]{:S(2)}) collective-permute-start(bf16[256,256]{1,0:T(8,128)(2,1)S(1)} %bitcast.4), channel_id=1, source_target_pairs={{0,1},{1,0},{2,3},{3,2},{4,5},{5,4},{6,7},{7,6},{8,9},{9,8},{10,11... | collective-permute-start | bytes 393224 | tf_op jit(solution)/shard_map/ppermute | solution.py:478
  25.5 11.0 %shard_map.113 = (bf16[4096,128]{1,0:T(8,128)(2,1)}, bf16[4096,128]{1,0:T(8,128)(2,1)}, f32[2,16,128]{2,1,0:T(8,128)S(1)}, f32[1,4096]{1,0:T(1,128)S(1)}, bf16[5...) custom-call(s32[2,8192]{1,0:T(2,128)S(1)} %get-tuple-element.19.rows_ref, ...), custom_call_target="tpu_custom_call" | custom-call | flops 4294967296 | bytes 1048576 | tf_op jit(solution)/shard_map/pallas_call | solution.py:49
  36.5 2.8 %collective-permute-start = (bf16[256,256]{1,0:T(8,128)(2,1)S(1)}, bf16[256,256]{1,0:T(8,128)(2,1)S(1)}, u32[]{:S(2)}, u32[]{:S(2)}) collective-permute-start(bf16[256,256]{1,0:T(8,128)(2,1)S(1)} %bitcast.5), channel_id=1, source_target_pairs={{0,2},{1,3},{2,0},{3,1},{4,6},{5,7},{6,4},{7,5},{8,10},{9,11},{10,... | collective-permute-start | bytes 393224 | tf_op jit(solution)/shard_map/ppermute | solution.py:478
  39.3 0.4 collective-permute-start.1
  39.7 0.2 collective-permute-start.3
  39.9 2.8 %collective-permute-start.4 = (bf16[256,256]{1,0:T(8,128)(2,1)S(1)}, bf16[256,256]{1,0:T(8,128)(2,1)S(1)}, u32[]{:S(2)}, u32[]{:S(2)}) collective-permute-start(bf16[256,256]{1,0:T(8,128)(2,1)S(1)} %bitcast.10), channel_id=1, source_target_pairs={{0,2},{1,3},{2,0},{3,1},{4,6},{5,7},{6,4},{7,5},{8,10},{9,11},{10,... | collective-permute-start | bytes 393224 | tf_op jit(solution)/shard_map/ppermute | solution.py:478
  42.7 0.0 collective-permute-done.2.flip.flip_1
  42.7 0.7 collective-permute-start.5
  43.4 6.2 %shard_map.114.done_ref = bf16[16,16,128]{2,1,0:T(8,128)(2,1)S(1)} custom-call(bf16[4096,256]{1,0:T(8,128)(2,1)} %embed_hbm.5, bf16[256,256]{1,0:T(8,128)(2,1)S(1)} %bitcast.7, bf16[256,256]{1,0:T(8,128)(2,1)S(1)} %collective-permute-done.2.flip.flip_1, bf16[4096,128]{1,0:T(8,128)(2,1)} %get-tuple-element.20.weight, f32[1,4096]{1,0:T(1,128)S(1)} %get-tuple-element.21.norms_ref), custom_call_target="tpu_custom_call" | custom-call | flops 2147483648 | bytes 1048576 | tf_op jit(solution)/shard_map/pallas_call | solution.py:49
  49.6 0.0 collective-permute-done.flip_2
  49.6 0.0 collective-permute-done.1.flip_3
  49.6 6.9 %shard_map.115.after = bf16[32,16,128]{2,1,0:T(8,128)(2,1)} custom-call(bf16[4096,256]{1,0:T(8,128)(2,1)} %embed_hbm.5, bf16[256,256]{1,0:T(8,128)(2,1)S(1)} %collective-permute-done.flip_2, bf16[256,256]{1,0:T(8,128)(2,1)S(1)} %collective-permute-done.1.flip_3, bf16[4096,128]{1,0:T(8,128)(2,1)} %get-tuple-element.20.weight, ...), custom_call_target="tpu_custom_call" | custom-call | flops 2147483648 | bytes 1048576 | tf_op jit(solution)/shard_map/pallas_call | solution.py:49
  56.5 4.6 %all-to-all-start.1 = ((bf16[32,16,128]{2,1,0:T(8,128)(2,1)}), bf16[32,16,128]{2,1,0:T(8,128)(2,1)S(1)}, u32[]{:S(2)}, u32[]{:S(2)}) async-start(bf16[32,16,128]{2,1,0:T(8,128)(2,1)} %shard_map.115.after), calls=%async_computation.1 | async-start | bytes 262144 | tf_op jit(solution)/shard_map/all_to_all | solution.py:456
  61.1 0.0 collective-permute-done.3.flip_1
  61.1 0.0 collective-permute-done.4.flip_2
  61.2 0.0 collective-permute-done.5.flip_3
  61.2 10.2 %shard_map.116.second_ref = bf16[32,16,128]{2,1,0:T(8,128)(2,1)S(1)} custom-call(bf16[4096,256]{1,0:T(8,128)(2,1)} %embed_hbm.5, bf16[256,256]{1,0:T(8,128)(2,1)S(1)} %bitcast.12, bf16[256,256]{1,0:T(8,128)(2,1)S(1)} %collective-permute-done.3.flip_1, bf16[256,256]{1,0:T(8,128)(2,1)S(1)} %collective-permute-done.4.flip_2, ...), custom_call_target="tpu_custom_call" | custom-call | flops 4294967296 | bytes 1048576 | tf_op jit(solution)/shard_map/pallas_call | solution.py:49
  71.4 0.5 all-to-all-done.1.arrived_ref
  71.9 0.7 shard_map.117.after
  72.6 9.3 %all-to-all-start.2 = ((bf16[32,32,128]{2,1,0:T(8,128)(2,1)}), bf16[32,32,128]{2,1,0:T(8,128)(2,1)S(1)}, u32[]{:S(2)}, u32[]{:S(2)}) async-start(bf16[32,32,128]{2,1,0:T(8,128)(2,1)} %shard_map.117.after), calls=%async_computation.2 | async-start | bytes 524288 | tf_op jit(solution)/shard_map/all_to_all | solution.py:456
  81.9 7.6 %shard_map.118 = (bf16[256,1024]{1,0:T(8,128)(2,1)S(1)}, f32[1024,128]{1,0:T(8,128)S(1)}) custom-call(s32[2,8192]{1,0:T(2,128)S(1)} %get-tuple-element.19.rows_ref, bf16[256,256]{1,0:T(8,128)(2,1)S(1)} %bitcast.8, bf16[256,256]{1,0:T(8,128)(2,1)S(1)} %collective-permute-done.2.flip.flip_1, bf16[256,256]{1,0:T(8,128)(2,1)S(1)} %collective-permute-done.flip_2, ...), custom_call_target="tpu_custom_call" | custom-call | flops 2147483648 | bytes 1048576 | tf_op jit(solution)/shard_map/pallas_call | solution.py:49
  89.5 5.3 %all-to-all-done.2.arrived_ref = bf16[32,32,128]{2,1,0:T(8,128)(2,1)S(1)} async-done(((bf16[32,32,128]{2,1,0:T(8,128)(2,1)}), bf16[32,32,128]{2,1,0:T(8,128)(2,1)S(1)}, u32[]{:S(2)}, u32[]{:S(2)}) %all-to-all-start.2) | async-done | bytes 262176 | tf_op jit(solution)/shard_map/all_to_all | solution.py:456
  94.9 1.2 shard_map.119.after
  96.0 4.2 %all-to-all-start.3 = ((bf16[8,144,128]{2,1,0:T(8,128)(2,1)}), bf16[8,144,128]{2,1,0:T(8,128)(2,1)S(1)}, u32[]{:S(2)}, u32[]{:S(2)}) async-start(bf16[8,144,128]{2,1,0:T(8,128)(2,1)} %shard_map.119.after), calls=%async_computation.3 | async-start | bytes 589824 | tf_op jit(solution)/shard_map/all_to_all | solution.py:456
  100.3 0.0 copy-start
  100.3 0.0 copy-start.1
  100.3 2.3 %shard_map.120.near = bf16[1024,512]{1,0:T(8,128)(2,1)S(1)} custom-call(bf16[1024,256]{1,0:T(8,128)(2,1)} %library_hbm.5, bf16[512,256]{1,0:T(8,128)(2,1)S(1)} %get-tuple-element.24.picks, bf16[8,144,128]{2,1,0:T(8,128)(2,1)} %shard_map.119.after), custom_call_target="tpu_custom_call" | custom-call | flops 536870912 | bytes 1048576 | tf_op jit(solution)/shard_map/pallas_call | solution.py:49
  102.6 0.0 copy-start.2
  102.6 4.6 %all-to-all-done.3.arrived_ref = bf16[8,144,128]{2,1,0:T(8,128)(2,1)S(1)} async-done(((bf16[8,144,128]{2,1,0:T(8,128)(2,1)}), bf16[8,144,128]{2,1,0:T(8,128)(2,1)S(1)}, u32[]{:S(2)}, u32[]{:S(2)}) %all-to-all-start.3) | async-done | bytes 294944 | tf_op jit(solution)/shard_map/all_to_all | solution.py:456
  107.2 1.2 shard_map.121
  108.4 6.3 %all-to-all-start.4 = ((bf16[32,16,128]{2,1,0:T(8,128)(2,1)}), bf16[32,16,128]{2,1,0:T(8,128)(2,1)S(1)}, u32[]{:S(2)}, u32[]{:S(2)}) async-start(bf16[32,16,128]{2,1,0:T(8,128)(2,1)} %get-tuple-element.32), calls=%async_computation.4 | async-start | bytes 262144 | tf_op jit(solution)/shard_map/all_to_all | solution.py:456
  114.7 0.0 copy-done
  114.8 0.0 copy-done.1
  114.8 3.4 %shard_map.122 = (f32[33,4096]{1,0:T(8,128)}, f32[33,4096]{1,0:T(8,128)}) custom-call(f32[512,64]{1,0:T(8,128)S(1)} %get-tuple-element.29.resid_ref, s32[128,16]{1,0:T(8,128)S(1)} %get-tuple-element.25.local_ref, f32[33,4096]{1,0:T(8,128)S(1)} %copy-done, f32[33,4096]{1,0:T(8,128)S(1)} %copy-done.1), custom_call_target="tpu_custom_call" | custom-call | bytes 1048576 | tf_op jit(solution)/shard_map/pallas_call | solution.py:49
  118.1 7.3 %all-to-all-done.4.arrived_ref = bf16[32,16,128]{2,1,0:T(8,128)(2,1)S(1)} async-done(((bf16[32,16,128]{2,1,0:T(8,128)(2,1)}), bf16[32,16,128]{2,1,0:T(8,128)(2,1)S(1)}, u32[]{:S(2)}, u32[]{:S(2)}) %all-to-all-start.4) | async-done | bytes 131104 | tf_op jit(solution)/shard_map/all_to_all | solution.py:456
  125.5 0.0 copy-done.2
  125.5 0.8 shard_map.123
  (1 shorter events, 0.0 us)
Async XLA Ops:
  23.1 19.6 %collective-permute-start.2 = (bf16[256,256]{1,0:T(8,128)(2,1)S(1)}, bf16[256,256]{1,0:T(8,128)(2,1)S(1)}, u32[]{:S(2)}, u32[]{:S(2)}) collective-permute-start(bf16[256,256]{1,0:T(8,128)(2,1)S(1)} %bitcast.4), channel_id=1, source_target_pairs={{0,1},{1,0},{2,3},{3,2},{4,5},{5,4},{6,7},{7,6},{8,9},{9,8},{10,11... | collective-permute-start | bytes 393224 | tf_op jit(solution)/shard_map/ppermute | solution.py:478
  36.5 13.1 %collective-permute-start = (bf16[256,256]{1,0:T(8,128)(2,1)S(1)}, bf16[256,256]{1,0:T(8,128)(2,1)S(1)}, u32[]{:S(2)}, u32[]{:S(2)}) collective-permute-start(bf16[256,256]{1,0:T(8,128)(2,1)S(1)} %bitcast.5), channel_id=1, source_target_pairs={{0,2},{1,3},{2,0},{3,1},{4,6},{5,7},{6,4},{7,5},{8,10},{9,11},{10,... | collective-permute-start | bytes 393224 | tf_op jit(solution)/shard_map/ppermute | solution.py:478
  39.3 10.3 %collective-permute-start.1 = (bf16[256,256]{1,0:T(8,128)(2,1)S(1)}, bf16[256,256]{1,0:T(8,128)(2,1)S(1)}, u32[]{:S(2)}, u32[]{:S(2)}) collective-permute-start(bf16[256,256]{1,0:T(8,128)(2,1)S(1)} %bitcast.6), channel_id=1, source_target_pairs={{0,3},{1,2},{2,1},{3,0},{4,7},{5,6},{6,5},{7,4},{8,11},{9,10},{10,... | collective-permute-start | bytes 393224 | tf_op jit(solution)/shard_map/ppermute | solution.py:478
  39.7 21.4 %collective-permute-start.3 = (bf16[256,256]{1,0:T(8,128)(2,1)S(1)}, bf16[256,256]{1,0:T(8,128)(2,1)S(1)}, u32[]{:S(2)}, u32[]{:S(2)}) collective-permute-start(bf16[256,256]{1,0:T(8,128)(2,1)S(1)} %bitcast.9), channel_id=1, source_target_pairs={{0,1},{1,0},{2,3},{3,2},{4,5},{5,4},{6,7},{7,6},{8,9},{9,8},{10,11... | collective-permute-start | bytes 393224 | tf_op jit(solution)/shard_map/ppermute | solution.py:478
  39.9 21.2 %collective-permute-start.4 = (bf16[256,256]{1,0:T(8,128)(2,1)S(1)}, bf16[256,256]{1,0:T(8,128)(2,1)S(1)}, u32[]{:S(2)}, u32[]{:S(2)}) collective-permute-start(bf16[256,256]{1,0:T(8,128)(2,1)S(1)} %bitcast.10), channel_id=1, source_target_pairs={{0,2},{1,3},{2,0},{3,1},{4,6},{5,7},{6,4},{7,5},{8,10},{9,11},{10,... | collective-permute-start | bytes 393224 | tf_op jit(solution)/shard_map/ppermute | solution.py:478
  42.7 18.5 %collective-permute-start.5 = (bf16[256,256]{1,0:T(8,128)(2,1)S(1)}, bf16[256,256]{1,0:T(8,128)(2,1)S(1)}, u32[]{:S(2)}, u32[]{:S(2)}) collective-permute-start(bf16[256,256]{1,0:T(8,128)(2,1)S(1)} %bitcast.11), channel_id=1, source_target_pairs={{0,3},{1,2},{2,1},{3,0},{4,7},{5,6},{6,5},{7,4},{8,11},{9,10},{10,... | collective-permute-start | bytes 393224 | tf_op jit(solution)/shard_map/ppermute | solution.py:478
  56.5 15.3 %all-to-all-start.1 = ((bf16[32,16,128]{2,1,0:T(8,128)(2,1)}), bf16[32,16,128]{2,1,0:T(8,128)(2,1)S(1)}, u32[]{:S(2)}, u32[]{:S(2)}) async-start(bf16[32,16,128]{2,1,0:T(8,128)(2,1)} %shard_map.115.after), calls=%async_computation.1 | async-start | bytes 262144 | tf_op jit(solution)/shard_map/all_to_all | solution.py:456
  72.6 22.2 %all-to-all-start.2 = ((bf16[32,32,128]{2,1,0:T(8,128)(2,1)}), bf16[32,32,128]{2,1,0:T(8,128)(2,1)S(1)}, u32[]{:S(2)}, u32[]{:S(2)}) async-start(bf16[32,32,128]{2,1,0:T(8,128)(2,1)} %shard_map.117.after), calls=%async_computation.2 | async-start | bytes 524288 | tf_op jit(solution)/shard_map/all_to_all | solution.py:456
  96.0 11.1 %all-to-all-start.3 = ((bf16[8,144,128]{2,1,0:T(8,128)(2,1)}), bf16[8,144,128]{2,1,0:T(8,128)(2,1)S(1)}, u32[]{:S(2)}, u32[]{:S(2)}) async-start(bf16[8,144,128]{2,1,0:T(8,128)(2,1)} %shard_map.119.after), calls=%async_computation.3 | async-start | bytes 589824 | tf_op jit(solution)/shard_map/all_to_all | solution.py:456
  100.3 14.5 %copy-start = (f32[33,4096]{1,0:T(8,128)S(1)}, f32[33,4096]{1,0:T(8,128)}, u32[]{:S(2)}) copy-start(f32[33,4096]{1,0:T(8,128)} %coef_ref.1) | copy-start | bytes 1622020
  100.3 14.5 %copy-start.1 = (f32[33,4096]{1,0:T(8,128)S(1)}, f32[33,4096]{1,0:T(8,128)}, u32[]{:S(2)}) copy-start(f32[33,4096]{1,0:T(8,128)} %vel_ref.1) | copy-start | bytes 1622020
  102.6 22.9 %copy-start.2 = (f32[32,32]{1,0:T(8,128)S(1)}, f32[32,32]{1,0:T(8,128)}, u32[]{:S(2)}) copy-start(f32[32,32]{1,0:T(8,128)} %prior_ref.1) | copy-start | bytes 12292
  108.4 17.1 %all-to-all-start.4 = ((bf16[32,16,128]{2,1,0:T(8,128)(2,1)}), bf16[32,16,128]{2,1,0:T(8,128)(2,1)S(1)}, u32[]{:S(2)}, u32[]{:S(2)}) async-start(bf16[32,16,128]{2,1,0:T(8,128)(2,1)} %get-tuple-element.32), calls=%async_computation.4 | async-start | bytes 262144 | tf_op jit(solution)/shard_map/all_to_all | solution.py:456

commit v2 on v1

--- a/solution.py
+++ b/solution.py
@@ -36,7 +36,8 @@
     spec = {"H": pl.BlockSpec(memory_space=pltpu.HBM), "V": pl.BlockSpec(memory_space=pltpu.VMEM)}
     spec["P"] = spec["V"]
     spec["A"] = pl.BlockSpec(memory_space=pl.ANY)
-    space = {"H": pltpu.HBM, "V": pltpu.VMEM, "P": pltpu.HBM, "A": pl.ANY}
+    spec["W"] = spec["V"]
+    space = {"H": pltpu.HBM, "V": pltpu.VMEM, "P": pltpu.HBM, "A": pl.ANY, "W": pl.ANY}
     kernel = pl.pallas_call(
         body,
         out_shape=[space[kind](shape, dtype) for kind, shape, dtype in outs],
@@ -289,28 +290,26 @@
         for copy in chunk(index):
             copy.wait()
 
-    rows = query.shape[0] // len(pieces)
-    fetches = [
-        pltpu.make_async_copy(piece, query.at[pl.ds(rows * index, rows)], sems.at[16 + index])
-        for index, piece in enumerate(pieces)
-    ]
-    for fetch in fetches:
-        fetch.start()
     for index in range(count):
         for copy in chunk(index):
             copy.start()
+    rows = query.shape[0] // len(pieces)
     if start_hbm is None:
         total[...] = jnp.zeros_like(total)
+        for index, piece in enumerate(pieces):
+            part = slice(rows * index, rows * index + rows)
+            query_norms[part, :] = norms_down(piece[...])
+            query[part, :] = piece[...] * bf16(-2)
     else:
-        fetch_start = pltpu.make_async_copy(start_hbm, total, sems.at[17])
-        fetch_start.start()
-    if between is not None:
+        fetches = [
+            pltpu.make_async_copy(pieces[0], query, sems.at[16]), pltpu.make_async_copy(start_hbm, total, sems.at[17])
+        ]
+        for fetch in fetches:
+            fetch.start()
         between()
-    for index, fetch in enumerate(fetches):
-        fetch.wait()
-        scaled(query, query_norms, slice(rows * index, rows * index + rows))
-    if start_hbm is not None:
-        fetch_start.wait()
+        for fetch in fetches:
+            fetch.wait()
+        scaled(query, query_norms, slice(0, rows))
     sweep(embed, query, weight, query_norms, cross, total, norms_ref, tiles, wait, short)
     return total
 
@@ -323,13 +322,13 @@
 
 def dense_rest_body(embed, flip_2, flip_3, weight, norms_ref, done_ref, out_ref, *scratch):
     train = places()[1]
-    total = dense(embed, [flip_2, flip_3], weight, norms_ref, scratch, (0, 8))
-    pack_flipped(total, train, (2, 3), out_ref)
     own = lax.rem(train, 4)
     for index in range(2):
         other = lax.bitwise_xor(own, index)
         for z in range(8):
             out_ref[4 * z + other] = done_ref[8 * index + z]
+    total = dense(embed, [flip_2, flip_3], weight, norms_ref, scratch, (0, 8))
+    pack_flipped(total, train, (2, 3), out_ref)
 
 
 def dense_second_body(embed, flip_0, flip_1, flip_2, flip_3, weight, norms_ref, after, out_ref, *scratch):
@@ -498,18 +497,18 @@
     )
     part_half = call(
         dense_first_body,
-        [("H", train_embed), ("A", flips[0][0]), ("A", flips[0][1]), ("H", ahead), ("V", norms)],
+        [("H", train_embed), ("W", flips[0][0]), ("W", flips[0][1]), ("H", ahead), ("V", norms)],
         [("V", (16, 16, 128), bf16)], dense_scratch(512), flops // 2,
     )
     part_0 = call(
         dense_rest_body,
-        [("H", train_embed), ("A", flips[0][2]), ("A", flips[0][3]), ("H", ahead), ("V", norms), ("V", part_half)],
+        [("H", train_embed), ("W", flips[0][2]), ("W", flips[0][3]), ("H", ahead), ("V", norms), ("V", part_half)],
         [block], dense_scratch(512), flops // 2,
     )
     arrived_0 = exchange(part_0, "train")
     part_1 = call(
         dense_second_body,
-        [("H", train_embed), *[("A", part) for part in flips[1]], ("H", base), ("V", norms), ("H", part_0)],
+        [("H", train_embed), *[("W", part) for part in flips[1]], ("H", base), ("V", norms), ("H", part_0)],
         [("V", (32, 16, 128), bf16)], dense_scratch(QUERIES), flops,
     )
     sent_1 = call(first_body, [("V", arrived_0), ("V", own), ("V", part_1)], [("P", (32, 32, 128), bf16)])

time: 127 us -> 125 us (0.984)
  Pallas kernels: 54.3 us -> 53 us
    pallas_call x12, Pallas kernels: 54.3 us -> 53 us  [call(): kernel(*[pltpu.with_memory_space_constraint(array, space[kind]) for kind,...]
  transfers between devices with their start and end apart: 10 -> 10, of which waited for: 4 -> 4; matrix products, arithmetic and copies ran while one was open for 0% -> 0% of each run, Pallas kernels for 38% -> 37%
where the time goes in v2:
time: 125 us
  Pallas kernels  53 us (42%)
  starting transfers between devices  33.1 us (26%)
  blocking collectives  19.5 us (16%)
  waiting for transfers between devices  18.5 us (15%)
    pallas_call x12, Pallas kernels, call(): kernel(*[pltpu.with_memory_space_constraint(array, space[kind]) for kind,...  53 us
    all_to_all x4, starting transfers between devices, exchange(): return lax.all_to_all(x, axis, split_axis=0, concat_axis=0, tiled=True)  23.8 us
    all_to_all x1, blocking collectives, whole(): lax.all_to_all(sent, 'train', 0, 0, axis_index_groups=columns, tiled=True)  19.5 us
    all_to_all x4, waiting for transfers between devices, exchange(): return lax.all_to_all(x, axis, split_axis=0, concat_axis=0, tiled=True)  18.5 us
    ppermute x6, starting transfers between devices, whole(): lax.ppermute(own_part, 'train', [(t, t ^ flip) for t in range(32)])  9.34 us
  transfers between devices with their start and end apart: 10, of which 4 were waited for; matrix products, arithmetic and copies ran while one was open for 0% of the time, Pallas kernels for 37%

profile of v2, /device:TPU:1, one launch (start us, length us, event | category | flops | bytes accessed | tf_op | source)
XLA Modules:
  0.0 124.9 jit_solution(5625620514929062833)
XLA Ops:
  0.6 2.9 %shard_map.112 = (bf16[8,2,32,256]{3,2,1,0:T(8,128)(2,1)}, s32[2,8192]{1,0:T(2,128)S(1)}) custom-call(s32[2,8192]{1,0:T(2,128)} %rows_hbm.1, bf16[4096,256]{1,0:T(8,128)(2,1)} %embed_hbm.5), custom_call_target="tpu_custom_call" | custom-call | bytes 1048576 | tf_op jit(solution)/shard_map/pallas_call | solution.py:50
  3.6 19.5 %all_to_all.25 = bf16[8,2,32,256]{3,2,1,0:T(8,128)(2,1)S(1)} all-to-all(bf16[8,2,32,256]{3,2,1,0:T(8,128)(2,1)} %get-tuple-element.18), channel_id=1, replica_groups={{0,4,8,12,16,20,24,28},{1,5,9,13,17,21,25,29},{2,6,10,14,18,22,26,30},{..., dimensions={0} | all-to-all | bytes 524288 | tf_op jit(solution)/shard_map/all_to_all | solution.py:471
  23.1 2.4 %collective-permute-start.2 = (bf16[256,256]{1,0:T(8,128)(2,1)S(1)}, bf16[256,256]{1,0:T(8,128)(2,1)S(1)}, u32[]{:S(2)}, u32[]{:S(2)}) collective-permute-start(bf16[256,256]{1,0:T(8,128)(2,1)S(1)} %bitcast.4), channel_id=1, source_target_pairs={{0,1},{1,0},{2,3},{3,2},{4,5},{5,4},{6,7},{7,6},{8,9},{9,8},{10,11... | collective-permute-start | bytes 393224 | tf_op jit(solution)/shard_map/ppermute | solution.py:477
  25.5 11.0 %shard_map.113 = (bf16[4096,128]{1,0:T(8,128)(2,1)}, bf16[4096,128]{1,0:T(8,128)(2,1)}, f32[2,16,128]{2,1,0:T(8,128)S(1)}, f32[1,4096]{1,0:T(1,128)S(1)}, bf16[5...) custom-call(s32[2,8192]{1,0:T(2,128)S(1)} %get-tuple-element.19.rows_ref, ...), custom_call_target="tpu_custom_call" | custom-call | flops 4294967296 | bytes 1048576 | tf_op jit(solution)/shard_map/pallas_call | solution.py:50
  36.5 2.8 %collective-permute-start = (bf16[256,256]{1,0:T(8,128)(2,1)S(1)}, bf16[256,256]{1,0:T(8,128)(2,1)S(1)}, u32[]{:S(2)}, u32[]{:S(2)}) collective-permute-start(bf16[256,256]{1,0:T(8,128)(2,1)S(1)} %bitcast.5), channel_id=1, source_target_pairs={{0,2},{1,3},{2,0},{3,1},{4,6},{5,7},{6,4},{7,5},{8,10},{9,11},{10,... | collective-permute-start | bytes 393224 | tf_op jit(solution)/shard_map/ppermute | solution.py:477
  39.3 0.4 collective-permute-start.1
  39.7 0.2 collective-permute-start.3
  39.9 2.8 %collective-permute-start.4 = (bf16[256,256]{1,0:T(8,128)(2,1)S(1)}, bf16[256,256]{1,0:T(8,128)(2,1)S(1)}, u32[]{:S(2)}, u32[]{:S(2)}) collective-permute-start(bf16[256,256]{1,0:T(8,128)(2,1)S(1)} %bitcast.10), channel_id=1, source_target_pairs={{0,2},{1,3},{2,0},{3,1},{4,6},{5,7},{6,4},{7,5},{8,10},{9,11},{10,... | collective-permute-start | bytes 393224 | tf_op jit(solution)/shard_map/ppermute | solution.py:477
  42.7 0.0 collective-permute-done.2.flip.flip_1
  42.7 0.7 collective-permute-start.5
  43.4 5.9 %shard_map.114.done_ref = bf16[16,16,128]{2,1,0:T(8,128)(2,1)S(1)} custom-call(bf16[4096,256]{1,0:T(8,128)(2,1)} %embed_hbm.5, bf16[256,256]{1,0:T(8,128)(2,1)S(1)} %bitcast.7, bf16[256,256]{1,0:T(8,128)(2,1)S(1)} %collective-permute-done.2.flip.flip_1, bf16[4096,128]{1,0:T(8,128)(2,1)} %get-tuple-element.20.weight, f32[1,4096]{1,0:T(1,128)S(1)} %get-tuple-element.21.norms_ref), custom_call_target="tpu_custom_call" | custom-call | flops 2147483648 | bytes 1048576 | tf_op jit(solution)/shard_map/pallas_call | solution.py:50
  49.3 0.0 collective-permute-done.flip_2
  49.3 0.0 collective-permute-done.1.flip_3
  49.3 6.6 %shard_map.115.after = bf16[32,16,128]{2,1,0:T(8,128)(2,1)} custom-call(bf16[4096,256]{1,0:T(8,128)(2,1)} %embed_hbm.5, bf16[256,256]{1,0:T(8,128)(2,1)S(1)} %collective-permute-done.flip_2, bf16[256,256]{1,0:T(8,128)(2,1)S(1)} %collective-permute-done.1.flip_3, bf16[4096,128]{1,0:T(8,128)(2,1)} %get-tuple-element.20.weight, ...), custom_call_target="tpu_custom_call" | custom-call | flops 2147483648 | bytes 1048576 | tf_op jit(solution)/shard_map/pallas_call | solution.py:50
  55.9 4.6 %all-to-all-start.1 = ((bf16[32,16,128]{2,1,0:T(8,128)(2,1)}), bf16[32,16,128]{2,1,0:T(8,128)(2,1)S(1)}, u32[]{:S(2)}, u32[]{:S(2)}) async-start(bf16[32,16,128]{2,1,0:T(8,128)(2,1)} %shard_map.115.after), calls=%async_computation.1 | async-start | bytes 262144 | tf_op jit(solution)/shard_map/all_to_all | solution.py:455
  60.5 0.0 collective-permute-done.3.flip_1
  60.5 0.0 collective-permute-done.4.flip_2
  60.5 0.0 collective-permute-done.5.flip_3
  60.5 9.5 %shard_map.116.second_ref = bf16[32,16,128]{2,1,0:T(8,128)(2,1)S(1)} custom-call(bf16[4096,256]{1,0:T(8,128)(2,1)} %embed_hbm.5, bf16[256,256]{1,0:T(8,128)(2,1)S(1)} %bitcast.12, bf16[256,256]{1,0:T(8,128)(2,1)S(1)} %collective-permute-done.3.flip_1, bf16[256,256]{1,0:T(8,128)(2,1)S(1)} %collective-permute-done.4.flip_2, ...), custom_call_target="tpu_custom_call" | custom-call | flops 4294967296 | bytes 1048576 | tf_op jit(solution)/shard_map/pallas_call | solution.py:50
  70.1 1.2 all-to-all-done.1.arrived_ref
  71.2 0.7 shard_map.117.after
  72.0 8.6 %all-to-all-start.2 = ((bf16[32,32,128]{2,1,0:T(8,128)(2,1)}), bf16[32,32,128]{2,1,0:T(8,128)(2,1)S(1)}, u32[]{:S(2)}, u32[]{:S(2)}) async-start(bf16[32,32,128]{2,1,0:T(8,128)(2,1)} %shard_map.117.after), calls=%async_computation.2 | async-start | bytes 524288 | tf_op jit(solution)/shard_map/all_to_all | solution.py:455
  80.6 7.6 %shard_map.118 = (bf16[256,1024]{1,0:T(8,128)(2,1)S(1)}, f32[1024,128]{1,0:T(8,128)S(1)}) custom-call(s32[2,8192]{1,0:T(2,128)S(1)} %get-tuple-element.19.rows_ref, bf16[256,256]{1,0:T(8,128)(2,1)S(1)} %bitcast.8, bf16[256,256]{1,0:T(8,128)(2,1)S(1)} %collective-permute-done.2.flip.flip_1, bf16[256,256]{1,0:T(8,128)(2,1)S(1)} %collective-permute-done.flip_2, ...), custom_call_target="tpu_custom_call" | custom-call | flops 2147483648 | bytes 1048576 | tf_op jit(solution)/shard_map/pallas_call | solution.py:50
  88.2 5.3 %all-to-all-done.2.arrived_ref = bf16[32,32,128]{2,1,0:T(8,128)(2,1)S(1)} async-done(((bf16[32,32,128]{2,1,0:T(8,128)(2,1)}), bf16[32,32,128]{2,1,0:T(8,128)(2,1)S(1)}, u32[]{:S(2)}, u32[]{:S(2)}) %all-to-all-start.2) | async-done | bytes 262176 | tf_op jit(solution)/shard_map/all_to_all | solution.py:455
  93.6 1.2 shard_map.119.after
  94.7 4.2 %all-to-all-start.3 = ((bf16[8,144,128]{2,1,0:T(8,128)(2,1)}), bf16[8,144,128]{2,1,0:T(8,128)(2,1)S(1)}, u32[]{:S(2)}, u32[]{:S(2)}) async-start(bf16[8,144,128]{2,1,0:T(8,128)(2,1)} %shard_map.119.after), calls=%async_computation.3 | async-start | bytes 589824 | tf_op jit(solution)/shard_map/all_to_all | solution.py:455
  99.0 0.0 copy-start
  99.0 0.0 copy-start.1
  99.0 2.3 %shard_map.120.near = bf16[1024,512]{1,0:T(8,128)(2,1)S(1)} custom-call(bf16[1024,256]{1,0:T(8,128)(2,1)} %library_hbm.5, bf16[512,256]{1,0:T(8,128)(2,1)S(1)} %get-tuple-element.24.picks, bf16[8,144,128]{2,1,0:T(8,128)(2,1)} %shard_map.119.after), custom_call_target="tpu_custom_call" | custom-call | flops 536870912 | bytes 1048576 | tf_op jit(solution)/shard_map/pallas_call | solution.py:50
  101.3 0.0 copy-start.2
  101.3 4.6 %all-to-all-done.3.arrived_ref = bf16[8,144,128]{2,1,0:T(8,128)(2,1)S(1)} async-done(((bf16[8,144,128]{2,1,0:T(8,128)(2,1)}), bf16[8,144,128]{2,1,0:T(8,128)(2,1)S(1)}, u32[]{:S(2)}, u32[]{:S(2)}) %all-to-all-start.3) | async-done | bytes 294944 | tf_op jit(solution)/shard_map/all_to_all | solution.py:455
  105.9 1.2 shard_map.121
  107.1 6.3 %all-to-all-start.4 = ((bf16[32,16,128]{2,1,0:T(8,128)(2,1)}), bf16[32,16,128]{2,1,0:T(8,128)(2,1)S(1)}, u32[]{:S(2)}, u32[]{:S(2)}) async-start(bf16[32,16,128]{2,1,0:T(8,128)(2,1)} %get-tuple-element.32), calls=%async_computation.4 | async-start | bytes 262144 | tf_op jit(solution)/shard_map/all_to_all | solution.py:455
  113.4 0.0 copy-done
  113.5 0.0 copy-done.1
  113.5 3.4 %shard_map.122 = (f32[33,4096]{1,0:T(8,128)}, f32[33,4096]{1,0:T(8,128)}) custom-call(f32[512,64]{1,0:T(8,128)S(1)} %get-tuple-element.29.resid_ref, s32[128,16]{1,0:T(8,128)S(1)} %get-tuple-element.25.local_ref, f32[33,4096]{1,0:T(8,128)S(1)} %copy-done, f32[33,4096]{1,0:T(8,128)S(1)} %copy-done.1), custom_call_target="tpu_custom_call" | custom-call | bytes 1048576 | tf_op jit(solution)/shard_map/pallas_call | solution.py:50
  116.8 7.3 %all-to-all-done.4.arrived_ref = bf16[32,16,128]{2,1,0:T(8,128)(2,1)S(1)} async-done(((bf16[32,16,128]{2,1,0:T(8,128)(2,1)}), bf16[32,16,128]{2,1,0:T(8,128)(2,1)S(1)}, u32[]{:S(2)}, u32[]{:S(2)}) %all-to-all-start.4) | async-done | bytes 131104 | tf_op jit(solution)/shard_map/all_to_all | solution.py:455
  124.2 0.0 copy-done.2
  124.2 0.8 shard_map.123
  (1 shorter events, 0.0 us)
Async XLA Ops:
  23.1 19.6 %collective-permute-start.2 = (bf16[256,256]{1,0:T(8,128)(2,1)S(1)}, bf16[256,256]{1,0:T(8,128)(2,1)S(1)}, u32[]{:S(2)}, u32[]{:S(2)}) collective-permute-start(bf16[256,256]{1,0:T(8,128)(2,1)S(1)} %bitcast.4), channel_id=1, source_target_pairs={{0,1},{1,0},{2,3},{3,2},{4,5},{5,4},{6,7},{7,6},{8,9},{9,8},{10,11... | collective-permute-start | bytes 393224 | tf_op jit(solution)/shard_map/ppermute | solution.py:477
  36.5 12.8 %collective-permute-start = (bf16[256,256]{1,0:T(8,128)(2,1)S(1)}, bf16[256,256]{1,0:T(8,128)(2,1)S(1)}, u32[]{:S(2)}, u32[]{:S(2)}) collective-permute-start(bf16[256,256]{1,0:T(8,128)(2,1)S(1)} %bitcast.5), channel_id=1, source_target_pairs={{0,2},{1,3},{2,0},{3,1},{4,6},{5,7},{6,4},{7,5},{8,10},{9,11},{10,... | collective-permute-start | bytes 393224 | tf_op jit(solution)/shard_map/ppermute | solution.py:477
  39.3 10.0 %collective-permute-start.1 = (bf16[256,256]{1,0:T(8,128)(2,1)S(1)}, bf16[256,256]{1,0:T(8,128)(2,1)S(1)}, u32[]{:S(2)}, u32[]{:S(2)}) collective-permute-start(bf16[256,256]{1,0:T(8,128)(2,1)S(1)} %bitcast.6), channel_id=1, source_target_pairs={{0,3},{1,2},{2,1},{3,0},{4,7},{5,6},{6,5},{7,4},{8,11},{9,10},{10,... | collective-permute-start | bytes 393224 | tf_op jit(solution)/shard_map/ppermute | solution.py:477
  39.7 20.8 %collective-permute-start.3 = (bf16[256,256]{1,0:T(8,128)(2,1)S(1)}, bf16[256,256]{1,0:T(8,128)(2,1)S(1)}, u32[]{:S(2)}, u32[]{:S(2)}) collective-permute-start(bf16[256,256]{1,0:T(8,128)(2,1)S(1)} %bitcast.9), channel_id=1, source_target_pairs={{0,1},{1,0},{2,3},{3,2},{4,5},{5,4},{6,7},{7,6},{8,9},{9,8},{10,11... | collective-permute-start | bytes 393224 | tf_op jit(solution)/shard_map/ppermute | solution.py:477
  39.9 20.6 %collective-permute-start.4 = (bf16[256,256]{1,0:T(8,128)(2,1)S(1)}, bf16[256,256]{1,0:T(8,128)(2,1)S(1)}, u32[]{:S(2)}, u32[]{:S(2)}) collective-permute-start(bf16[256,256]{1,0:T(8,128)(2,1)S(1)} %bitcast.10), channel_id=1, source_target_pairs={{0,2},{1,3},{2,0},{3,1},{4,6},{5,7},{6,4},{7,5},{8,10},{9,11},{10,... | collective-permute-start | bytes 393224 | tf_op jit(solution)/shard_map/ppermute | solution.py:477
  42.7 17.9 %collective-permute-start.5 = (bf16[256,256]{1,0:T(8,128)(2,1)S(1)}, bf16[256,256]{1,0:T(8,128)(2,1)S(1)}, u32[]{:S(2)}, u32[]{:S(2)}) collective-permute-start(bf16[256,256]{1,0:T(8,128)(2,1)S(1)} %bitcast.11), channel_id=1, source_target_pairs={{0,3},{1,2},{2,1},{3,0},{4,7},{5,6},{6,5},{7,4},{8,11},{9,10},{10,... | collective-permute-start | bytes 393224 | tf_op jit(solution)/shard_map/ppermute | solution.py:477
  55.9 15.3 %all-to-all-start.1 = ((bf16[32,16,128]{2,1,0:T(8,128)(2,1)}), bf16[32,16,128]{2,1,0:T(8,128)(2,1)S(1)}, u32[]{:S(2)}, u32[]{:S(2)}) async-start(bf16[32,16,128]{2,1,0:T(8,128)(2,1)} %shard_map.115.after), calls=%async_computation.1 | async-start | bytes 262144 | tf_op jit(solution)/shard_map/all_to_all | solution.py:455
  72.0 21.6 %all-to-all-start.2 = ((bf16[32,32,128]{2,1,0:T(8,128)(2,1)}), bf16[32,32,128]{2,1,0:T(8,128)(2,1)S(1)}, u32[]{:S(2)}, u32[]{:S(2)}) async-start(bf16[32,32,128]{2,1,0:T(8,128)(2,1)} %shard_map.117.after), calls=%async_computation.2 | async-start | bytes 524288 | tf_op jit(solution)/shard_map/all_to_all | solution.py:455
  94.7 11.1 %all-to-all-start.3 = ((bf16[8,144,128]{2,1,0:T(8,128)(2,1)}), bf16[8,144,128]{2,1,0:T(8,128)(2,1)S(1)}, u32[]{:S(2)}, u32[]{:S(2)}) async-start(bf16[8,144,128]{2,1,0:T(8,128)(2,1)} %shard_map.119.after), calls=%async_computation.3 | async-start | bytes 589824 | tf_op jit(solution)/shard_map/all_to_all | solution.py:455
  99.0 14.5 %copy-start = (f32[33,4096]{1,0:T(8,128)S(1)}, f32[33,4096]{1,0:T(8,128)}, u32[]{:S(2)}) copy-start(f32[33,4096]{1,0:T(8,128)} %coef_ref.1) | copy-start | bytes 1622020
  99.0 14.5 %copy-start.1 = (f32[33,4096]{1,0:T(8,128)S(1)}, f32[33,4096]{1,0:T(8,128)}, u32[]{:S(2)}) copy-start(f32[33,4096]{1,0:T(8,128)} %vel_ref.1) | copy-start | bytes 1622020
  101.3 22.9 %copy-start.2 = (f32[32,32]{1,0:T(8,128)S(1)}, f32[32,32]{1,0:T(8,128)}, u32[]{:S(2)}) copy-start(f32[32,32]{1,0:T(8,128)} %prior_ref.1) | copy-start | bytes 12292
  107.1 17.1 %all-to-all-start.4 = ((bf16[32,16,128]{2,1,0:T(8,128)(2,1)}), bf16[32,16,128]{2,1,0:T(8,128)(2,1)S(1)}, u32[]{:S(2)}, u32[]{:S(2)}) async-start(bf16[32,16,128]{2,1,0:T(8,128)(2,1)} %get-tuple-element.32), calls=%async_computation.4 | async-start | bytes 262144 | tf_op jit(solution)/shard_map/all_to_all | solution.py:455

commit v3 on v2

--- a/solution.py
+++ b/solution.py
@@ -108,6 +108,24 @@
 
 def one_below_other(x):
     return jnp.concatenate([x[:, 0:HALF], x[:, HALF:]], axis=0)
+
+
+def tight(x):
+    bands = [x[8 * band : 8 * band + 8] for band in range(4)]
+    main = jnp.concatenate([band[:, 0:32] for band in bands], axis=1)
+    last = jnp.concatenate([*[band[:, 32:33] for band in bands], jnp.zeros((8, 124), f32)], axis=1)
+    return main, last
+
+
+def loose(main, last):
+    rest = jnp.zeros((8, 31), f32)
+    return jnp.concatenate(
+        [
+            jnp.concatenate([main[:, 32 * band : 32 * band + 32], last[:, band : band + 1], rest], axis=1)
+            for band in range(4)
+        ],
+        axis=0,
+    )
 
 
 def pack(total, out_ref):
@@ -334,7 +352,13 @@
 def dense_second_body(embed, flip_0, flip_1, flip_2, flip_3, weight, norms_ref, after, out_ref, *scratch):
     del after
     total = dense(embed, [flip_0, flip_1, flip_2, flip_3], weight, norms_ref, scratch, (0, 8))
-    pack_flipped(total, places()[1], range(4), out_ref)
+    own = lax.rem(places()[1], 4)
+    for flip in range(4):
+        other = lax.bitwise_xor(own, flip)
+        for z in range(8):
+            start = 256 * flip + 32 * z
+            main, last = tight(SCALE * total[start : start + 32, 0:HALF])
+            out_ref[4 * z + other] = jnp.concatenate([main, last], axis=0)
 
 
 def between_body(
@@ -385,29 +409,36 @@
     total = own_ref[0]
     for place in range(32):
         total = total + arrived_ref[place].astype(f32)
-    total = total.astype(bf16)
+    main, last = tight(one_below_other(total))
+    lane = lax.broadcasted_iota(jnp.int32, (8, 128), 1)
     for place in range(32):
-        out_ref[place, 0:16, :] = total
-        out_ref[place, 16:32, :] = second_ref[place]
+        other = pltpu.roll(second_ref[place, 8:16, :], 4, axis=1)
+        out_ref[place] = jnp.concatenate(
+            [main, second_ref[place, 0:8, :], jnp.where(lane < 4, last, other)], axis=0
+        ).astype(bf16)
 
 
 def second_body(arrived_ref, own_ref, between, out_ref, resid):
     batch, train = places()
-    total = own_ref[1]
+    mains = jnp.zeros((8, 128), f32)
+    lasts = jnp.zeros((8, 128), f32)
     for place in range(32):
-        total = total + arrived_ref[place, 16:32, :].astype(f32)
+        mains = mains + arrived_ref[place, 8:16, :].astype(f32)
+        lasts = lasts + arrived_ref[place, 16:24, :].astype(f32)
+    mine = one_below_other(own_ref[1]) + loose(mains, pltpu.roll(lasts, 124, axis=1))
     own = lax.rem(train, 4)
     for flip in range(4):
         other = lax.bitwise_xor(own, flip)
         for z in range(8):
             start = 256 * flip + 32 * z
-            resid[start : start + 32, :] = one_below_other(arrived_ref[4 * z + other, 0:16, :])
-    mine = one_below_other(total)
+            block = arrived_ref[4 * z + other].astype(f32)
+            resid[start : start + 32, :] = loose(block[0:8], block[16:24]).astype(bf16)
     change = dot_nn(between[...], resid[...]) * (-CUT * SCALE)
     group = lax.broadcasted_iota(jnp.int32, (256, HALF), 0) // 32
     change = change + jnp.where(group == batch, jnp.concatenate([mine] * 8, axis=0), 0.0)
     change = jnp.concatenate([change[0:128], change[128:256]], axis=1).astype(bf16)
-    kept = arrived_ref[train, 0:16, :]
+    kept = resid[pl.ds(pl.multiple_of((train // 4) * 32, 32), 32), :].astype(f32)
+    kept = side_by_side(kept).astype(bf16)
     for place in range(8):
         out_ref[place, 0:128, :] = change
         out_ref[place, 128:144, :] = kept
@@ -509,9 +540,9 @@
     part_1 = call(
         dense_second_body,
         [("H", train_embed), *[("W", part) for part in flips[1]], ("H", base), ("V", norms), ("H", part_0)],
-        [("V", (32, 16, 128), bf16)], dense_scratch(QUERIES), flops,
-    )
-    sent_1 = call(first_body, [("V", arrived_0), ("V", own), ("V", part_1)], [("P", (32, 32, 128), bf16)])
+        [("V", (32, 16, 128), f32)], dense_scratch(QUERIES), flops,
+    )
+    sent_1 = call(first_body, [("V", arrived_0), ("V", own), ("V", part_1)], [("P", (32, 24, 128), bf16)])
     arrived_1 = exchange(sent_1, "train")
     between, library = call(
         between_body,

time: 125 us -> 126 us (level)
  no operation moved by 1% of the time
where the time goes in v3:
time: 126 us; the launch traced here: 125 us
  Pallas kernels  53.2 us (42%)
  starting transfers between devices  34 us (27%)
  blocking collectives  19.5 us (15%)
  waiting for transfers between devices  17.6 us (14%)
    pallas_call x12, Pallas kernels, call(): kernel(*[pltpu.with_memory_space_constraint(array, space[kind]) for kind,...  53.2 us
    all_to_all x4, starting transfers between devices, exchange(): return lax.all_to_all(x, axis, split_axis=0, concat_axis=0, tiled=True)  24.7 us
    all_to_all x1, blocking collectives, whole(): lax.all_to_all(sent, 'train', 0, 0, axis_index_groups=columns, tiled=True)  19.5 us
    all_to_all x4, waiting for transfers between devices, exchange(): return lax.all_to_all(x, axis, split_axis=0, concat_axis=0, tiled=True)  17.6 us
    ppermute x6, starting transfers between devices, whole(): lax.ppermute(own_part, 'train', [(t, t ^ flip) for t in range(32)])  9.34 us
  transfers between devices with their start and end apart: 10, of which 4 were waited for; matrix products, arithmetic and copies ran while one was open for 0% of the time, Pallas kernels for 37%

profile of v3, /device:TPU:1, one launch (start us, length us, event | category | flops | bytes accessed | tf_op | source)
XLA Modules:
  0.0 125.1 jit_solution(9519253559461478494)
XLA Ops:
  0.6 2.9 %shard_map.112 = (bf16[8,2,32,256]{3,2,1,0:T(8,128)(2,1)}, s32[2,8192]{1,0:T(2,128)S(1)}) custom-call(s32[2,8192]{1,0:T(2,128)} %rows_hbm.1, bf16[4096,256]{1,0:T(8,128)(2,1)} %embed_hbm.5), custom_call_target="tpu_custom_call" | custom-call | bytes 1048576 | tf_op jit(solution)/shard_map/pallas_call | solution.py:50
  3.6 19.5 %all_to_all.25 = bf16[8,2,32,256]{3,2,1,0:T(8,128)(2,1)S(1)} all-to-all(bf16[8,2,32,256]{3,2,1,0:T(8,128)(2,1)} %get-tuple-element.18), channel_id=1, replica_groups={{0,4,8,12,16,20,24,28},{1,5,9,13,17,21,25,29},{2,6,10,14,18,22,26,30},{..., dimensions={0} | all-to-all | bytes 524288 | tf_op jit(solution)/shard_map/all_to_all | solution.py:502
  23.1 2.4 %collective-permute-start.2 = (bf16[256,256]{1,0:T(8,128)(2,1)S(1)}, bf16[256,256]{1,0:T(8,128)(2,1)S(1)}, u32[]{:S(2)}, u32[]{:S(2)}) collective-permute-start(bf16[256,256]{1,0:T(8,128)(2,1)S(1)} %bitcast.4), channel_id=1, source_target_pairs={{0,1},{1,0},{2,3},{3,2},{4,5},{5,4},{6,7},{7,6},{8,9},{9,8},{10,11... | collective-permute-start | bytes 393224 | tf_op jit(solution)/shard_map/ppermute | solution.py:508
  25.5 11.0 %shard_map.113 = (bf16[4096,128]{1,0:T(8,128)(2,1)}, bf16[4096,128]{1,0:T(8,128)(2,1)}, f32[2,16,128]{2,1,0:T(8,128)S(1)}, f32[1,4096]{1,0:T(1,128)S(1)}, bf16[5...) custom-call(s32[2,8192]{1,0:T(2,128)S(1)} %get-tuple-element.19.rows_ref, ...), custom_call_target="tpu_custom_call" | custom-call | flops 4294967296 | bytes 1048576 | tf_op jit(solution)/shard_map/pallas_call | solution.py:50
  36.5 2.8 %collective-permute-start = (bf16[256,256]{1,0:T(8,128)(2,1)S(1)}, bf16[256,256]{1,0:T(8,128)(2,1)S(1)}, u32[]{:S(2)}, u32[]{:S(2)}) collective-permute-start(bf16[256,256]{1,0:T(8,128)(2,1)S(1)} %bitcast.5), channel_id=1, source_target_pairs={{0,2},{1,3},{2,0},{3,1},{4,6},{5,7},{6,4},{7,5},{8,10},{9,11},{10,... | collective-permute-start | bytes 393224 | tf_op jit(solution)/shard_map/ppermute | solution.py:508
  39.3 0.4 collective-permute-start.1
  39.7 0.2 collective-permute-start.3
  39.9 2.8 %collective-permute-start.4 = (bf16[256,256]{1,0:T(8,128)(2,1)S(1)}, bf16[256,256]{1,0:T(8,128)(2,1)S(1)}, u32[]{:S(2)}, u32[]{:S(2)}) collective-permute-start(bf16[256,256]{1,0:T(8,128)(2,1)S(1)} %bitcast.10), channel_id=1, source_target_pairs={{0,2},{1,3},{2,0},{3,1},{4,6},{5,7},{6,4},{7,5},{8,10},{9,11},{10,... | collective-permute-start | bytes 393224 | tf_op jit(solution)/shard_map/ppermute | solution.py:508
  42.7 0.0 collective-permute-done.2.flip.flip_1
  42.7 0.7 collective-permute-start.5
  43.4 5.9 %shard_map.114.done_ref = bf16[16,16,128]{2,1,0:T(8,128)(2,1)S(1)} custom-call(bf16[4096,256]{1,0:T(8,128)(2,1)} %embed_hbm.5, bf16[256,256]{1,0:T(8,128)(2,1)S(1)} %bitcast.7, bf16[256,256]{1,0:T(8,128)(2,1)S(1)} %collective-permute-done.2.flip.flip_1, bf16[4096,128]{1,0:T(8,128)(2,1)} %get-tuple-element.20.weight, f32[1,4096]{1,0:T(1,128)S(1)} %get-tuple-element.21.norms_ref), custom_call_target="tpu_custom_call" | custom-call | flops 2147483648 | bytes 1048576 | tf_op jit(solution)/shard_map/pallas_call | solution.py:50
  49.3 0.0 collective-permute-done.flip_2
  49.3 0.0 collective-permute-done.1.flip_3
  49.3 6.6 %shard_map.115.after = bf16[32,16,128]{2,1,0:T(8,128)(2,1)} custom-call(bf16[4096,256]{1,0:T(8,128)(2,1)} %embed_hbm.5, bf16[256,256]{1,0:T(8,128)(2,1)S(1)} %collective-permute-done.flip_2, bf16[256,256]{1,0:T(8,128)(2,1)S(1)} %collective-permute-done.1.flip_3, bf16[4096,128]{1,0:T(8,128)(2,1)} %get-tuple-element.20.weight, ...), custom_call_target="tpu_custom_call" | custom-call | flops 2147483648 | bytes 1048576 | tf_op jit(solution)/shard_map/pallas_call | solution.py:50
  55.9 4.6 %all-to-all-start.1 = ((bf16[32,16,128]{2,1,0:T(8,128)(2,1)}), bf16[32,16,128]{2,1,0:T(8,128)(2,1)S(1)}, u32[]{:S(2)}, u32[]{:S(2)}) async-start(bf16[32,16,128]{2,1,0:T(8,128)(2,1)} %shard_map.115.after), calls=%async_computation.1 | async-start | bytes 262144 | tf_op jit(solution)/shard_map/all_to_all | solution.py:486
  60.5 0.0 collective-permute-done.3.flip_1
  60.5 0.0 collective-permute-done.4.flip_2
  60.5 0.0 collective-permute-done.5.flip_3
  60.5 9.6 %shard_map.116.second_ref = f32[32,16,128]{2,1,0:T(8,128)S(1)} custom-call(bf16[4096,256]{1,0:T(8,128)(2,1)} %embed_hbm.5, bf16[256,256]{1,0:T(8,128)(2,1)S(1)} %bitcast.12, bf16[256,256]{1,0:T(8,128)(2,1)S(1)} %collective-permute-done.3.flip_1, bf16[256,256]{1,0:T(8,128)(2,1)S(1)} %collective-permute-done.4.flip_2, ...), custom_call_target="tpu_custom_call" | custom-call | flops 4294967296 | bytes 1048576 | tf_op jit(solution)/shard_map/pallas_call | solution.py:50
  70.1 1.1 all-to-all-done.1.arrived_ref
  71.2 0.9 shard_map.117.after
  72.1 8.7 %all-to-all-start.2 = ((bf16[32,24,128]{2,1,0:T(8,128)(2,1)}), bf16[32,24,128]{2,1,0:T(8,128)(2,1)S(1)}, u32[]{:S(2)}, u32[]{:S(2)}) async-start(bf16[32,24,128]{2,1,0:T(8,128)(2,1)} %shard_map.117.after), calls=%async_computation.2 | async-start | bytes 393216 | tf_op jit(solution)/shard_map/all_to_all | solution.py:486
  80.8 7.6 %shard_map.118 = (bf16[256,1024]{1,0:T(8,128)(2,1)S(1)}, f32[1024,128]{1,0:T(8,128)S(1)}) custom-call(s32[2,8192]{1,0:T(2,128)S(1)} %get-tuple-element.19.rows_ref, bf16[256,256]{1,0:T(8,128)(2,1)S(1)} %bitcast.8, bf16[256,256]{1,0:T(8,128)(2,1)S(1)} %collective-permute-done.2.flip.flip_1, bf16[256,256]{1,0:T(8,128)(2,1)S(1)} %collective-permute-done.flip_2, ...), custom_call_target="tpu_custom_call" | custom-call | flops 2147483648 | bytes 1048576 | tf_op jit(solution)/shard_map/pallas_call | solution.py:50
  88.4 4.2 %all-to-all-done.2.arrived_ref = bf16[32,24,128]{2,1,0:T(8,128)(2,1)S(1)} async-done(((bf16[32,24,128]{2,1,0:T(8,128)(2,1)}), bf16[32,24,128]{2,1,0:T(8,128)(2,1)S(1)}, u32[]{:S(2)}, u32[]{:S(2)}) %all-to-all-start.2) | async-done | bytes 196640 | tf_op jit(solution)/shard_map/all_to_all | solution.py:486
  92.6 1.2 shard_map.119.after
  93.8 4.2 %all-to-all-start.3 = ((bf16[8,144,128]{2,1,0:T(8,128)(2,1)}), bf16[8,144,128]{2,1,0:T(8,128)(2,1)S(1)}, u32[]{:S(2)}, u32[]{:S(2)}) async-start(bf16[8,144,128]{2,1,0:T(8,128)(2,1)} %shard_map.119.after), calls=%async_computation.3 | async-start | bytes 589824 | tf_op jit(solution)/shard_map/all_to_all | solution.py:486
  98.0 0.0 copy-start
  98.1 0.0 copy-start.1
  98.1 2.3 %shard_map.120.near = bf16[1024,512]{1,0:T(8,128)(2,1)S(1)} custom-call(bf16[1024,256]{1,0:T(8,128)(2,1)} %library_hbm.5, bf16[512,256]{1,0:T(8,128)(2,1)S(1)} %get-tuple-element.24.picks, bf16[8,144,128]{2,1,0:T(8,128)(2,1)} %shard_map.119.after), custom_call_target="tpu_custom_call" | custom-call | flops 536870912 | bytes 1048576 | tf_op jit(solution)/shard_map/pallas_call | solution.py:50
  100.3 0.0 copy-start.2
  100.4 4.9 %all-to-all-done.3.arrived_ref = bf16[8,144,128]{2,1,0:T(8,128)(2,1)S(1)} async-done(((bf16[8,144,128]{2,1,0:T(8,128)(2,1)}), bf16[8,144,128]{2,1,0:T(8,128)(2,1)S(1)}, u32[]{:S(2)}, u32[]{:S(2)}) %all-to-all-start.3) | async-done | bytes 294944 | tf_op jit(solution)/shard_map/all_to_all | solution.py:486
  105.2 1.2 shard_map.121
  106.5 7.2 %all-to-all-start.4 = ((bf16[32,16,128]{2,1,0:T(8,128)(2,1)}), bf16[32,16,128]{2,1,0:T(8,128)(2,1)S(1)}, u32[]{:S(2)}, u32[]{:S(2)}) async-start(bf16[32,16,128]{2,1,0:T(8,128)(2,1)} %get-tuple-element.32), calls=%async_computation.4 | async-start | bytes 262144 | tf_op jit(solution)/shard_map/all_to_all | solution.py:486
  113.7 0.0 copy-done
  113.7 0.0 copy-done.1
  113.7 3.4 %shard_map.122 = (f32[33,4096]{1,0:T(8,128)}, f32[33,4096]{1,0:T(8,128)}) custom-call(f32[512,64]{1,0:T(8,128)S(1)} %get-tuple-element.29.resid_ref, s32[128,16]{1,0:T(8,128)S(1)} %get-tuple-element.25.local_ref, f32[33,4096]{1,0:T(8,128)S(1)} %copy-done, f32[33,4096]{1,0:T(8,128)S(1)} %copy-done.1), custom_call_target="tpu_custom_call" | custom-call | bytes 1048576 | tf_op jit(solution)/shard_map/pallas_call | solution.py:50
  117.0 7.3 %all-to-all-done.4.arrived_ref = bf16[32,16,128]{2,1,0:T(8,128)(2,1)S(1)} async-done(((bf16[32,16,128]{2,1,0:T(8,128)(2,1)}), bf16[32,16,128]{2,1,0:T(8,128)(2,1)S(1)}, u32[]{:S(2)}, u32[]{:S(2)}) %all-to-all-start.4) | async-done | bytes 131104 | tf_op jit(solution)/shard_map/all_to_all | solution.py:486
  124.4 0.0 copy-done.2
  124.4 0.8 shard_map.123
  (1 shorter events, 0.0 us)
Async XLA Ops:
  23.1 19.6 %collective-permute-start.2 = (bf16[256,256]{1,0:T(8,128)(2,1)S(1)}, bf16[256,256]{1,0:T(8,128)(2,1)S(1)}, u32[]{:S(2)}, u32[]{:S(2)}) collective-permute-start(bf16[256,256]{1,0:T(8,128)(2,1)S(1)} %bitcast.4), channel_id=1, source_target_pairs={{0,1},{1,0},{2,3},{3,2},{4,5},{5,4},{6,7},{7,6},{8,9},{9,8},{10,11... | collective-permute-start | bytes 393224 | tf_op jit(solution)/shard_map/ppermute | solution.py:508
  36.5 12.8 %collective-permute-start = (bf16[256,256]{1,0:T(8,128)(2,1)S(1)}, bf16[256,256]{1,0:T(8,128)(2,1)S(1)}, u32[]{:S(2)}, u32[]{:S(2)}) collective-permute-start(bf16[256,256]{1,0:T(8,128)(2,1)S(1)} %bitcast.5), channel_id=1, source_target_pairs={{0,2},{1,3},{2,0},{3,1},{4,6},{5,7},{6,4},{7,5},{8,10},{9,11},{10,... | collective-permute-start | bytes 393224 | tf_op jit(solution)/shard_map/ppermute | solution.py:508
  39.3 10.0 %collective-permute-start.1 = (bf16[256,256]{1,0:T(8,128)(2,1)S(1)}, bf16[256,256]{1,0:T(8,128)(2,1)S(1)}, u32[]{:S(2)}, u32[]{:S(2)}) collective-permute-start(bf16[256,256]{1,0:T(8,128)(2,1)S(1)} %bitcast.6), channel_id=1, source_target_pairs={{0,3},{1,2},{2,1},{3,0},{4,7},{5,6},{6,5},{7,4},{8,11},{9,10},{10,... | collective-permute-start | bytes 393224 | tf_op jit(solution)/shard_map/ppermute | solution.py:508
  39.7 20.8 %collective-permute-start.3 = (bf16[256,256]{1,0:T(8,128)(2,1)S(1)}, bf16[256,256]{1,0:T(8,128)(2,1)S(1)}, u32[]{:S(2)}, u32[]{:S(2)}) collective-permute-start(bf16[256,256]{1,0:T(8,128)(2,1)S(1)} %bitcast.9), channel_id=1, source_target_pairs={{0,1},{1,0},{2,3},{3,2},{4,5},{5,4},{6,7},{7,6},{8,9},{9,8},{10,11... | collective-permute-start | bytes 393224 | tf_op jit(solution)/shard_map/ppermute | solution.py:508
  39.9 20.6 %collective-permute-start.4 = (bf16[256,256]{1,0:T(8,128)(2,1)S(1)}, bf16[256,256]{1,0:T(8,128)(2,1)S(1)}, u32[]{:S(2)}, u32[]{:S(2)}) collective-permute-start(bf16[256,256]{1,0:T(8,128)(2,1)S(1)} %bitcast.10), channel_id=1, source_target_pairs={{0,2},{1,3},{2,0},{3,1},{4,6},{5,7},{6,4},{7,5},{8,10},{9,11},{10,... | collective-permute-start | bytes 393224 | tf_op jit(solution)/shard_map/ppermute | solution.py:508
  42.7 17.9 %collective-permute-start.5 = (bf16[256,256]{1,0:T(8,128)(2,1)S(1)}, bf16[256,256]{1,0:T(8,128)(2,1)S(1)}, u32[]{:S(2)}, u32[]{:S(2)}) collective-permute-start(bf16[256,256]{1,0:T(8,128)(2,1)S(1)} %bitcast.11), channel_id=1, source_target_pairs={{0,3},{1,2},{2,1},{3,0},{4,7},{5,6},{6,5},{7,4},{8,11},{9,10},{10,... | collective-permute-start | bytes 393224 | tf_op jit(solution)/shard_map/ppermute | solution.py:508
  55.9 15.3 %all-to-all-start.1 = ((bf16[32,16,128]{2,1,0:T(8,128)(2,1)}), bf16[32,16,128]{2,1,0:T(8,128)(2,1)S(1)}, u32[]{:S(2)}, u32[]{:S(2)}) async-start(bf16[32,16,128]{2,1,0:T(8,128)(2,1)} %shard_map.115.after), calls=%async_computation.1 | async-start | bytes 262144 | tf_op jit(solution)/shard_map/all_to_all | solution.py:486
  72.1 20.5 %all-to-all-start.2 = ((bf16[32,24,128]{2,1,0:T(8,128)(2,1)}), bf16[32,24,128]{2,1,0:T(8,128)(2,1)S(1)}, u32[]{:S(2)}, u32[]{:S(2)}) async-start(bf16[32,24,128]{2,1,0:T(8,128)(2,1)} %shard_map.117.after), calls=%async_computation.2 | async-start | bytes 393216 | tf_op jit(solution)/shard_map/all_to_all | solution.py:486
  93.8 11.4 %all-to-all-start.3 = ((bf16[8,144,128]{2,1,0:T(8,128)(2,1)}), bf16[8,144,128]{2,1,0:T(8,128)(2,1)S(1)}, u32[]{:S(2)}, u32[]{:S(2)}) async-start(bf16[8,144,128]{2,1,0:T(8,128)(2,1)} %shard_map.119.after), calls=%async_computation.3 | async-start | bytes 589824 | tf_op jit(solution)/shard_map/all_to_all | solution.py:486
  98.0 15.6 %copy-start = (f32[33,4096]{1,0:T(8,128)S(1)}, f32[33,4096]{1,0:T(8,128)}, u32[]{:S(2)}) copy-start(f32[33,4096]{1,0:T(8,128)} %coef_ref.1) | copy-start | bytes 1622020
  98.1 15.6 %copy-start.1 = (f32[33,4096]{1,0:T(8,128)S(1)}, f32[33,4096]{1,0:T(8,128)}, u32[]{:S(2)}) copy-start(f32[33,4096]{1,0:T(8,128)} %vel_ref.1) | copy-start | bytes 1622020
  100.3 24.0 %copy-start.2 = (f32[32,32]{1,0:T(8,128)S(1)}, f32[32,32]{1,0:T(8,128)}, u32[]{:S(2)}) copy-start(f32[32,32]{1,0:T(8,128)} %prior_ref.1) | copy-start | bytes 12292
  106.5 17.9 %all-to-all-start.4 = ((bf16[32,16,128]{2,1,0:T(8,128)(2,1)}), bf16[32,16,128]{2,1,0:T(8,128)(2,1)S(1)}, u32[]{:S(2)}, u32[]{:S(2)}) async-start(bf16[32,16,128]{2,1,0:T(8,128)(2,1)} %get-tuple-element.32), calls=%async_computation.4 | async-start | bytes 262144 | tf_op jit(solution)/shard_map/all_to_all | solution.py:486
